TPU v7x, 256 devices: a whole 4x4x8 slice. The times are simulated.
256 devices in a mesh: chan: 16 (over z, x_lo), win: 16 (over x_hi, y, core).
Axes of the slice: x: 4 (x_hi: 2, x_lo: 2; x = x_hi * 2 + x_lo), y: 4, z: 8, core: 2. Of those that a mesh axis runs over, the one named last changes fastest.
Arguments:
- records: bfloat16 [512, 128, 2048], P('win', None, 'chan'), may hold values from -8 to 8
- fir_taps: float32 [64], replicated, may hold values from -0.75 to 0.75
Outputs:
- correlations: bfloat16 [128, 128, 1024], P('chan', 'win')
All inputs are finite; a program needn't handle non-finite values.
Results may differ from a plain program's by a relative error of at most 0.0038.
Values may be sent and summed in bfloat16 or wider, within the bound.
No kernel may reach another device: no remote copies, remote signals or barrier semaphores. Data moves between devices by JAX's collectives and lax.ppermute only.
A program may use at most 64 MiB of HBM per device.

v0:
```python
import math

import jax
import jax.numpy as jnp
from jax import lax
from jax.sharding import PartitionSpec as P

BAND = 512
FIRST_BIN = 16
LAGS = 512
HALF_WIDTH = 32
TAPS = 64


def phase_angles(rows, cols, length):
    product = jnp.mod(rows[:, None] * cols[None, :], length)
    return 2.0 * math.pi / length * product.astype(jnp.float32)


def forward_table(sample_idx, length):
    band_bins = FIRST_BIN + jnp.arange(BAND, dtype=jnp.int32)
    angles = phase_angles(sample_idx, band_bins, length)
    return jnp.concatenate([jnp.cos(angles), -jnp.sin(angles)], axis=1)


def smoother_matrix():
    ramp = jnp.arange(BAND, dtype=jnp.int32)
    offset = jnp.mod(ramp[:, None] - ramp[None, :], BAND)
    near = (offset <= HALF_WIDTH) | (offset >= BAND - HALF_WIDTH)
    return near.astype(jnp.float32)


def cross_parts(own_re, own_im, other_re, other_im):
    cross_re = jnp.einsum(
        "wif,wjf->ijf", own_re, other_re, preferred_element_type=jnp.float32
    ) + jnp.einsum("wif,wjf->ijf", own_im, other_im, preferred_element_type=jnp.float32)
    cross_im = jnp.einsum(
        "wif,wjf->ijf", own_im, other_re, preferred_element_type=jnp.float32
    ) - jnp.einsum("wif,wjf->ijf", own_re, other_im, preferred_element_type=jnp.float32)
    return (cross_re, cross_im)


def body(records, fir_taps):
    regrouped = lax.all_to_all(records, "chan", split_axis=1, concat_axis=2, tiled=True)
    win_dev, chan_dev, length = regrouped.shape
    fwd_table = forward_table(jnp.arange(length, dtype=jnp.int32), length)
    spectra = jnp.dot(
        regrouped.reshape(win_dev * chan_dev, length).astype(jnp.float32),
        fwd_table,
        precision=lax.Precision.HIGHEST,
        preferred_element_type=jnp.float32,
    )
    tap_table = forward_table(jnp.arange(TAPS, dtype=jnp.int32), length)
    response = jnp.dot(
        fir_taps[None, :],
        tap_table,
        precision=lax.Precision.HIGHEST,
        preferred_element_type=jnp.float32,
    )[0]
    spec_re = spectra[:, :BAND]
    spec_im = spectra[:, BAND:]
    resp_re = response[:BAND]
    resp_im = response[BAND:]
    filt_re = spec_re * resp_re - spec_im * resp_im
    filt_im = spec_re * resp_im + spec_im * resp_re
    smooth = jnp.dot(
        filt_re * filt_re + filt_im * filt_im,
        smoother_matrix(),
        precision=lax.Precision.HIGHEST,
        preferred_element_type=jnp.float32,
    ) / (2 * HALF_WIDTH + 1)
    inv_amp = 1.0 / jnp.sqrt(smooth + 1e-06)
    whitened = jnp.concatenate([filt_re * inv_amp, filt_im * inv_amp], axis=1).astype(jnp.bfloat16)
    whitened = whitened.reshape(win_dev, chan_dev, 2 * BAND)
    total_chan = chan_dev * lax.axis_size("chan")
    windows_all = win_dev * lax.axis_size("win")
    band_bins = FIRST_BIN + jnp.arange(BAND, dtype=jnp.int32)
    lag_steps = jnp.arange(2 * LAGS, dtype=jnp.int32) - LAGS
    angles = phase_angles(band_bins, lag_steps, length)
    inverse = jnp.concatenate([jnp.cos(angles), -jnp.sin(angles)], axis=0) / (windows_all * BAND)
    own_re = whitened[:, :, :BAND]
    own_im = whitened[:, :, BAND:]
    block_in = lax.all_gather(whitened, "chan", axis=1, tiled=True)
    cross_re, cross_im = cross_parts(own_re, own_im, block_in[:, :, :BAND], block_in[:, :, BAND:])
    joined = jnp.concatenate([cross_re, cross_im], axis=-1)
    lagged = jnp.dot(
        joined.reshape(chan_dev * total_chan, 2 * BAND),
        inverse,
        precision=lax.Precision.HIGHEST,
        preferred_element_type=jnp.float32,
    )
    lagged = lagged.reshape(chan_dev, total_chan, 2 * LAGS)
    summed = lax.psum_scatter(lagged, "win", scatter_dimension=1, tiled=True)
    return summed.astype(jnp.bfloat16)


def solution(mesh):
    in_specs = (P("win", None, "chan"), P())
    out_specs = P("chan", "win", None)
    return jax.shard_map(body, mesh=mesh, in_specs=in_specs, out_specs=out_specs, check_vma=False)
```

profile of v0, /device:TPU:1, one launch (start us, length us, event | category | flops | bytes accessed | tf_op | source)
XLA Modules:
  0.0 385.2 jit_solution(14828283479683274223)
XLA Ops:
  6.5 3.0 copy.13
  9.5 10.0 %all-to-all-start = ((bf16[32,128,128]{2,0,1:T(8,128)(2,1)}), bf16[32,128,128]{2,0,1:T(8,128)(2,1)S(1)}, u32[]{:S(2)}, u32[]{:S(2)}) async-start(bf16[32,128,128]{2,0,1:T(8,128)(2,1)} %copy.13), calls=%async_computation | async-start | bytes 2097152 | tf_op jit(solution)/shard_map/all_to_all | solution.py:44
  19.6 0.0 all-gather.2.cloned.1.call-start
  19.6 0.5 fusion.56
  20.2 0.3 fusion.46
  20.4 18.1 %fusion.20 = (f32[2048,512]{1,0:T(8,128)}, f32[2048,512]{1,0:T(8,128)}) fusion(s32[512]{0:T(512)S(1)} %iota_add_fusion.1), kind=kLoop, calls=%fused_computation.33 | loop fusion | flops 15728640 | bytes 8390656 | tf_op jit(solution)/shard_map/cos | solution.py:23
  38.5 6.4 %all-to-all-done = bf16[32,128,128]{2,0,1:T(8,128)(2,1)S(1)} async-done(((bf16[32,128,128]{2,0,1:T(8,128)(2,1)}), bf16[32,128,128]{2,0,1:T(8,128)(2,1)S(1)}, u32[]{:S(2)}, u32[]{:S(2)}) %all-to-all-start) | async-done | bytes 1048608 | tf_op jit(solution)/shard_map/all_to_all | solution.py:44
  44.9 0.7 copy.33
  45.5 7.6 %fusion.21 = f32[256,1024]{1,0:T(8,128)S(1)} fusion(f32[2048,512]{1,0:T(8,128)} %get-tuple-element.16, f32[2048,512]{1,0:T(8,128)} %get-tuple-element.15, bf16[32,8,16,128]{3,2,1,0:T(8,128)(2,1)S(1)} %bitcast.35), kind=kOutput, calls=%fused_computation.37 | convolution fusion | flops 6444548096 | bytes 10485760 | tf_op jit(solution)/shard_map/dot_general | solution.py:47
  53.2 1.2 fusion.44
  54.3 0.1 pad_maximum_fusion.1
  54.4 1.1 copy.15
  55.5 0.0 all-gather.2.cloned.1.call-update
  55.5 0.2 reduce-scatter.2.cloned.1.call-start
  55.8 9.8 %fusion.29 = (f32[512,1024]{1,0:T(8,128)}, f32[512,1024]{1,0:T(8,128)}) fusion(s32[1024]{0:T(1024)S(1)} %iota_add_fusion, s32[512]{0:T(512)S(1)} %iota_add_fusion.1), kind=kLoop, calls=%fused_computation.45 | loop fusion | flops 7864320 | bytes 4200448 | tf_op jit(solution)/shard_map/cos | solution.py:80
  65.5 0.8 copy.17
  66.4 0.8 copy.19
  67.2 171.4 %all-gather.2.cloned.1.call-done = bf16[32,128,1024]{2,0,1:T(8,128)(2,1)} async-done(((bf16[32,8,1024]{2,0,1:T(8,128)(2,1)}), bf16[32,128,1024]{2,0,1:T(8,128)(2,1)}) %all-gather.2.cloned.1.call-update) | async-done | bytes 8388624 | tf_op jit(solution)/shard_map/all_gather | solution.py:83
  238.7 6.0 %fusion.67 = (bf16[32,128,512]{2,0,1:T(8,128)(2,1)}, bf16[32,128,512]{2,0,1:T(8,128)(2,1)}) fusion(bf16[32,128,1024]{2,0,1:T(8,128)(2,1)} %all-gather.2.cloned.1.call-done), kind=kLoop, calls=%fused_computation.94 | loop fusion | bytes 16777216 | tf_op jit(solution)/shard_map/slice | solution.py:84
  244.7 9.1 %copy.23 = bf16[32,128,512]{1,0,2:T(8,128)(2,1)} copy(bf16[32,128,512]{2,0,1:T(8,128)(2,1)} %get-tuple-element.6) | data formatting | bytes 8388608
  253.8 9.1 %copy.24 = bf16[32,128,512]{1,0,2:T(8,128)(2,1)} copy(bf16[32,128,512]{2,0,1:T(8,128)(2,1)} %get-tuple-element.5) | data formatting | bytes 8388608
  263.0 3.5 fusion.73
  266.5 1.2 fusion.74
  267.8 1.0 copy-done.2
  268.7 1.2 add_bitcast_fusion
  270.0 1.2 subtract_bitcast_fusion
  271.2 0.3 pad_maximum_fusion
  271.5 1.3 copy-done.3
  272.8 0.6 copy-done.4
  273.4 15.2 %fusion.8 = f32[8,128,1024]{2,1,0:T(8,128)} fusion(f32[512,1024]{1,0:T(8,128)S(1)} %copy-done.4, f32[512,1024]{1,0:T(8,128)S(1)} %copy-done.3, f32[8,128,1024]{1,0,2:T(8,128)S(1)} %pad_maximum_fusion), kind=kOutput, calls=%fused_computation.13 | convolution fusion | flops 12886999040 | bytes 12582912 | tf_op jit(solution)/shard_map/dot_general | solution.py:86
  288.6 88.1 %reduce-scatter.2.cloned.1.call-done = f32[8,8,1024]{2,1,0:T(8,128)} async-done(((f32[8,128,1024]{2,1,0:T(8,128)}), f32[8,8,1024]{2,1,0:T(8,128)}) %reduce-scatter.2.cloned.1.call-update) | async-done | bytes 262160 | tf_op jit(solution)/shard_map/reduce_scatter | solution.py:93
  376.8 1.6 convert_element_type.25
  (11 shorter events, 0.0 us)
Async XLA Ops:
  6.5 13.6 %copy-start = (f32[64]{0:T(128)S(1)}, f32[64]{0:T(128)}, u32[]{:S(2)}) copy-start(f32[64]{0:T(128)} %param.3) | copy-start | bytes 772
  9.5 35.4 %all-to-all-start = ((bf16[32,128,128]{2,0,1:T(8,128)(2,1)}), bf16[32,128,128]{2,0,1:T(8,128)(2,1)S(1)}, u32[]{:S(2)}, u32[]{:S(2)}) async-start(bf16[32,128,128]{2,0,1:T(8,128)(2,1)} %copy.13), calls=%async_computation | async-start | bytes 2097152 | tf_op jit(solution)/shard_map/all_to_all | solution.py:44
  19.6 219.1 %all-gather.2.cloned.1.call-start = ((), (), s32[]{:S(2)}) async-start(), calls=%async_computation.2 | async-start | bytes 8912896 | tf_op jit(solution)/shard_map/all_gather | solution.py:83
  55.5 321.2 %reduce-scatter.2.cloned.1.call-start = ((), (), s32[]{:S(2)}) async-start(), calls=%async_computation.3 | async-start | bytes 4456448 | tf_op jit(solution)/shard_map/reduce_scatter | solution.py:93
  263.0 3.5 copy-start.1
  266.5 2.2 copy-start.2
  271.2 1.6 copy-start.3
  271.2 2.2 copy-start.4
Sparse Core Ops, SparseCore 0:
  55.6 182.9 all-gather.1
  288.8 87.9 reduce-scatter.1
where the time goes:
time: 386 us; the launch traced here: 385 us
  waiting for transfers between devices  266 us (69%)
  local copies, waits for them, and re-layouts  33.7 us (9%)
  matrix products  31.4 us (8%)
  other arithmetic  30.3 us (8%)
  between operations  13.5 us (3%)
  starting transfers between devices  10.3 us (3%)
    all_gather x1, waiting for transfers between devices, body(): block_in = lax.all_gather(whitened, 'chan', axis=1, tiled=True)  171 us
    reduce_scatter x1, waiting for transfers between devices, body(): summed = lax.psum_scatter(lagged, 'win', scatter_dimension=1, tiled=True)  88.1 us
    unnamed x13, local copies, waits for them, and re-layouts  24.1 us
    cos x2, other arithmetic, forward_table(): return jnp.concatenate([jnp.cos(angles), -jnp.sin(angles)], axis=1)  18.6 us
    dot_general x1, matrix products, body(): jnp.dot(joined.reshape(chan_dev * total_chan, 2 * BAND), inverse, precisi...  15.2 us
    all_to_all x1, starting transfers between devices, body(): lax.all_to_all(records, 'chan', split_axis=1, concat_axis=2, tiled=True)  10 us
    cos x1, other arithmetic, body(): jnp.cos(angles)  9.77 us
  transfers between devices with their start and end apart: 3, of which 3 were waited for; matrix products, arithmetic and copies ran while one was open for 8% of the time, Pallas kernels for 0%

commit v1 on v0

v1 whole, which is shorter than its diff:
```python
import functools
import math

import jax
import jax.numpy as jnp
import ml_dtypes
import numpy as np
from jax import lax
from jax.experimental import pallas as pl
from jax.experimental.pallas import tpu as pltpu
from jax.sharding import PartitionSpec as P

LENGTH = 2048
BAND = 512
FIRST_BIN = 16
LAGS = 512
HALF_WIDTH = 32
TAPS = 64
CHANNELS = 128
WINDOWS = 512
BOTH = ("chan", "win")

BF16 = jnp.bfloat16
F32 = jnp.float32


def split_table(table):
    hi = table.astype(ml_dtypes.bfloat16)
    lo = (table - hi.astype(np.float64)).astype(ml_dtypes.bfloat16)
    return hi, lo


def phases(rows, cols):
    return 2.0 * math.pi / LENGTH * np.mod(rows[:, None] * cols[None, :], LENGTH).astype(np.float64)


@functools.cache
def tables():
    bins = FIRST_BIN + np.arange(BAND)
    angles = phases(bins, np.arange(LENGTH))
    forward = np.concatenate([np.cos(angles), -np.sin(angles)], axis=0)
    offset = np.mod(np.arange(BAND)[:, None] - np.arange(BAND)[None, :], BAND)
    near = (offset <= HALF_WIDTH) | (offset >= BAND - HALF_WIDTH)
    angles = phases(bins, np.arange(2 * LAGS) - LAGS)
    inverse = np.stack([np.cos(angles), -np.sin(angles)], axis=1) / (WINDOWS * BAND)
    inverse = inverse.reshape(BAND // 2, 2, 2, 2 * LAGS).transpose(1, 0, 2, 3).reshape(2 * BAND, 2 * LAGS)
    taps = forward[:, :TAPS].astype(np.float32)
    return split_table(forward), near.astype(ml_dtypes.bfloat16), split_table(inverse), taps


def dot_nt(a, b):
    return lax.dot_general(a, b, (((1,), (1,)), ((), ())), preferred_element_type=F32)


def dot_tn(a, b):
    return lax.dot_general(a, b, (((0,), (0,)), ((), ())), preferred_element_type=F32)


def dot_nn(a, b):
    return jnp.dot(a, b, preferred_element_type=F32)


def swap_halves(low, high, bit, shift, axis):
    size = low.shape[axis]
    new_low = jnp.where(bit, pltpu.roll(high, shift, axis), low)
    new_high = jnp.where(bit, high, pltpu.roll(low, size - shift, axis))
    return new_low, new_high


def whiten_kernel(y_ref, hi_ref, lo_ref, resp_ref, near_ref, out_ref, acc_ref):
    step = pl.program_id(0)
    blocks = y_ref.shape[0]
    x = jnp.concatenate([y_ref[s] for s in range(blocks)], axis=1)
    part = dot_nt(hi_ref[...], x) + dot_nt(lo_ref[...], x)

    @pl.when(step == 0)
    def _():
        acc_ref[...] = part

    @pl.when(step > 0)
    def _():
        acc_ref[...] += part

    @pl.when(step == pl.num_programs(0) - 1)
    def _():
        resp_re = jnp.concatenate([resp_ref[:BAND]] * 2, axis=1)
        resp_im = jnp.concatenate([resp_ref[BAND:]] * 2, axis=1)
        spec_re = acc_ref[:BAND]
        spec_im = acc_ref[BAND:]
        filt_re = spec_re * resp_re - spec_im * resp_im
        filt_im = spec_re * resp_im + spec_im * resp_re
        power = filt_re * filt_re + filt_im * filt_im
        first = power.astype(BF16)
        rest = power - first.astype(F32)
        second = rest.astype(BF16)
        third = (rest - second.astype(F32)).astype(BF16)
        near = near_ref[...]
        smooth = (dot_nn(near, first) + dot_nn(near, second) + dot_nn(near, third)) / (2 * HALF_WIDTH + 1)
        inv_amp = 1.0 / jnp.sqrt(smooth + 1e-06)
        white_re = filt_re * inv_amp
        white_im = filt_im * inv_amp
        half = CHANNELS
        a = [white_re[:, :half], white_re[:, half:], white_im[:, :half], white_im[:, half:]]
        row = lax.broadcasted_iota(jnp.int32, a[0].shape, 0)
        top = (row & 4) != 0
        mid = (row & 2) != 0
        for k in (0, 1):
            a[k], a[k + 2] = swap_halves(a[k], a[k + 2], top, 4, 0)
        for k in (0, 2):
            a[k], a[k + 1] = swap_halves(a[k], a[k + 1], mid, 2, 0)
        for k in range(4):
            out_ref[:, k] = a[k].reshape(BAND // 8, 8, CHANNELS).astype(BF16)


def cross_kernel(b_ref, out_ref):
    b = b_ref[...]
    wide = b.astype(F32)
    rows = wide.shape[0]
    row = lax.broadcasted_iota(jnp.int32, wide.shape, 0)
    imag = (row & 4) != 0
    odd = (row & 1) != 0
    turned = jnp.where(imag, pltpu.roll(wide, 4, 0), -pltpu.roll(wide, rows - 4, 0))
    zero = jnp.zeros_like(wide)
    columns = [
        jnp.where(odd, zero, wide),
        jnp.where(odd, wide, zero),
        jnp.where(odd, zero, turned),
        jnp.where(odd, turned, zero),
    ]
    z = jnp.concatenate([c.astype(BF16) for c in columns], axis=1)
    cross = dot_tn(b, z)
    row = lax.broadcasted_iota(jnp.int32, (CHANNELS, CHANNELS), 0)
    lane = lax.broadcasted_iota(jnp.int32, (CHANNELS, CHANNELS), 1)
    parts = [cross[:, k * CHANNELS : (k + 1) * CHANNELS] for k in range(4)]
    for down, right in ((4, 32), (2, 16), (1, 8)):
        row_bit = (row & down) != 0
        lane_bit = (lane & right) != 0
        for k in range(4):
            a = parts[k]
            up = pltpu.roll(pltpu.roll(a, CHANNELS - down, 0), right, 1)
            dn = pltpu.roll(pltpu.roll(a, down, 0), CHANNELS - right, 1)
            parts[k] = jnp.where(row_bit == lane_bit, a, jnp.where(row_bit, dn, up))
    lane_bit = (lane & 64) != 0
    for part in range(2):
        even, odd = swap_halves(parts[2 * part], parts[2 * part + 1], lane_bit, 64, 1)
        for high, a in enumerate((even, odd)):
            for c in range(CHANNELS // 8):
                start = c * 32 + high * 16 + part
                out_ref[pl.ds(start, 8, stride=2), :] = a[c * 8 : c * 8 + 8]


def lag_kernel(c_ref, hi_ref, lo_ref, out_ref):
    turned = c_ref[...].T
    lhs = jnp.concatenate([turned[:64], turned[64:]], axis=1)
    hi = lhs.astype(BF16)
    lo = (lhs - hi.astype(F32)).astype(BF16)
    total = dot_nn(hi, hi_ref[...]) + (dot_nn(lo, hi_ref[...]) + dot_nn(hi, lo_ref[...]))
    out_ref[...] = total.astype(BF16)


def body(records, fir_taps):
    (fwd_hi, fwd_lo), near, (inv_hi, inv_lo), taps_table = tables()
    y = lax.all_to_all(records, "chan", 0, 0, tiled=True)
    blocks = LENGTH // CHANNELS
    y = y.reshape(blocks, 2 * CHANNELS, CHANNELS)
    response = jnp.dot(
        taps_table,
        jnp.broadcast_to(fir_taps[:, None], (TAPS, 128)),
        precision=lax.Precision.HIGHEST,
        preferred_element_type=F32,
    )
    steps = 4
    depth = LENGTH // steps
    white = pl.pallas_call(
        whiten_kernel,
        grid=(steps,),
        in_specs=[
            pl.BlockSpec((blocks // steps, 2 * CHANNELS, CHANNELS), lambda s: (s, 0, 0)),
            pl.BlockSpec((2 * BAND, depth), lambda s: (0, s)),
            pl.BlockSpec((2 * BAND, depth), lambda s: (0, s)),
            pl.BlockSpec((2 * BAND, 128), lambda s: (0, 0)),
            pl.BlockSpec((BAND, BAND), lambda s: (0, 0)),
        ],
        out_specs=pl.BlockSpec((BAND // 8, 4, 8, CHANNELS), lambda s: (0, 0, 0, 0)),
        out_shape=jax.ShapeDtypeStruct((BAND // 8, 4, 8, CHANNELS), BF16),
        scratch_shapes=[pltpu.VMEM((2 * BAND, 2 * CHANNELS), F32)],
        name="whiten",
    )(y, fwd_hi, fwd_lo, response, near)
    owners = BAND // 2
    white = lax.all_to_all(white.reshape(owners, 8, CHANNELS), BOTH, 0, 0, tiled=True)
    cross = pl.pallas_call(
        cross_kernel,
        out_shape=jax.ShapeDtypeStruct((2 * owners, 128), F32),
        name="cross",
    )(white.reshape(owners * 8, CHANNELS))
    cross = lax.all_to_all(cross.reshape(owners, 2, 128), BOTH, 0, 0, tiled=True)
    lagged = pl.pallas_call(
        lag_kernel,
        out_shape=jax.ShapeDtypeStruct((64, 2 * LAGS), BF16),
        name="lag",
    )(cross.reshape(2 * owners, 128), inv_hi, inv_lo)
    return lagged.reshape(8, 8, 2 * LAGS)


def solution(mesh):
    in_specs = (P("win", None, "chan"), P())
    out_specs = P("chan", "win", None)
    return jax.shard_map(body, mesh=mesh, in_specs=in_specs, out_specs=out_specs, check_vma=False)
```

time: 386 us -> 109 us (0.28)
  waiting for transfers between devices: 266 us -> 22.8 us
  blocking collectives: 0 us -> 56.7 us
  local copies, waits for them, and re-layouts: 33.7 us -> 0.97 us
  other arithmetic: 30.3 us -> 0 us
  matrix products: 31.4 us -> 2.45 us
  Pallas kernels: 0 us -> 15.6 us
  between operations: 13.5 us -> 0.02 us
    all_gather x1 -> x0, waiting for transfers between devices: 171 us -> none  [body(): block_in = lax.all_gather(whitened, 'chan', axis=1, tiled=True)]
    reduce_scatter x1 -> x0, waiting for transfers between devices: 88.1 us -> none  [body(): summed = lax.psum_scatter(lagged, 'win', scatter_dimension=1, tiled=True)]
    all_to_all x0 -> x2, blocking collectives: none -> 56.7 us  [the longest x1 33.7 us: body(): lax.all_to_all(white.reshape(owners, 8, CHANNELS), BOTH, 0, 0, tiled=True)]
    dot_general x8 -> x1, matrix products: 31.4 us -> 2.45 us  [body(): jnp.dot(taps_table, jnp.broadcast_to(fir_taps[:, None], (TAPS, 128)), pre...]
    cos x3 -> x0, other arithmetic: 28.4 us -> none  [the longest x2 18.6 us: forward_table(): return jnp.concatenate([jnp.cos(angles), -jnp.sin(angles)], axis=1)]
    unnamed x13 -> x4, local copies, waits for them, and re-layouts: 24.1 us -> 0.97 us
    all_to_all x1, waiting for transfers between devices: 6.37 us -> 22.8 us  [body(): y = lax.all_to_all(records, 'chan', 0, 0, tiled=True)]
    pallas_call x0 -> x3, Pallas kernels: none -> 15.6 us  [the longest x1 8.57 us: body(): pl.pallas_call(whiten_kernel, grid=(steps,), in_specs=[pl.BlockSpec((bloc...]
  transfers between devices with their start and end apart: 3 -> 1, of which waited for: 3 -> 1; matrix products, arithmetic and copies ran while one was open for 8% -> 2% of each run, Pallas kernels for 0% -> 0%
where the time goes in v1:
time: 109 us
  blocking collectives  56.7 us (52%)
  waiting for transfers between devices  22.8 us (21%)
  Pallas kernels  15.6 us (14%)
  starting transfers between devices  10.2 us (9%)
  matrix products  2.45 us (2%)
    all_to_all x1, blocking collectives, body(): lax.all_to_all(white.reshape(owners, 8, CHANNELS), BOTH, 0, 0, tiled=True)  33.7 us
    all_to_all x1, blocking collectives, body(): lax.all_to_all(cross.reshape(owners, 2, 128), BOTH, 0, 0, tiled=True)  23 us
    all_to_all x1, waiting for transfers between devices, body(): y = lax.all_to_all(records, 'chan', 0, 0, tiled=True)  22.8 us
    all_to_all x1, starting transfers between devices, body(): y = lax.all_to_all(records, 'chan', 0, 0, tiled=True)  10.2 us
    pallas_call x1, Pallas kernels, body(): pl.pallas_call(whiten_kernel, grid=(steps,), in_specs=[pl.BlockSpec((bloc...  8.57 us
    pallas_call x1, Pallas kernels, body(): pl.pallas_call(lag_kernel, out_shape=jax.ShapeDtypeStruct((64, 2 * LAGS),...  4.21 us
    pallas_call x1, Pallas kernels, body(): pl.pallas_call(cross_kernel, out_shape=jax.ShapeDtypeStruct((2 * owners,...  2.84 us
    dot_general x1, matrix products, body(): jnp.dot(taps_table, jnp.broadcast_to(fir_taps[:, None], (TAPS, 128)), pre...  2.45 us
  transfers between devices with their start and end apart: 1, of which 1 were waited for; matrix products, arithmetic and copies ran while one was open for 2% of the time, Pallas kernels for 0%

profile of v1, /device:TPU:1, one launch (start us, length us, event | category | flops | bytes accessed | tf_op | source)
XLA Modules:
  0.0 108.8 jit_solution(9879329663330803093)
XLA Ops:
  0.0 0.0 copy-start
  0.0 10.2 %all-to-all-start = ((bf16[32,128,128]{2,1,0:T(8,128)(2,1)}), bf16[32,128,128]{2,1,0:T(8,128)(2,1)S(1)}, u32[]{:S(2)}, u32[]{:S(2)}) async-start(bf16[32,128,128]{2,1,0:T(8,128)(2,1)} %param.8), calls=%async_computation | async-start | bytes 2097152 | tf_op jit(solution)/shard_map/all_to_all | solution.py:163
  10.2 0.0 copy-done
  10.2 2.5 %fusion.resp_ref = f32[1024,128]{1,0:T(8,128)} fusion(f32[1024,64]{1,0:T(8,128)} %constant.12.clone, f32[64]{0:T(128)S(1)} %copy-done), kind=kOutput, calls=%fused_computation | convolution fusion | flops 100663296 | bytes 786688 | tf_op jit(solution)/shard_map/dot_general | solution.py:166
  12.7 22.8 %all-to-all-done = bf16[32,128,128]{2,1,0:T(8,128)(2,1)S(1)} async-done(((bf16[32,128,128]{2,1,0:T(8,128)(2,1)}), bf16[32,128,128]{2,1,0:T(8,128)(2,1)S(1)}, u32[]{:S(2)}, u32[]{:S(2)}) %all-to-all-start) | async-done | bytes 1048608 | tf_op jit(solution)/shard_map/all_to_all | solution.py:163
  35.5 0.0 copy-start.1
  35.5 1.0 copy-done.1
  36.5 8.6 %whiten.1 = bf16[64,4,8,128]{3,2,1,0:T(8,128)(2,1)} custom-call(bf16[16,256,128]{2,1,0:T(8,128)(2,1)} %bitcast.7, bf16[1024,2048]{1,0:T(8,128)(2,1)} %constant.13.clone.hi_ref, bf16[1024,2048]{1,0:T(8,128)(2,1)} %constant.14.clone.lo_ref, f32[1024,128]{1,0:T(8,128)} %fusion.resp_ref, bf16[512,512]{1,0:T(8,128)(2,1)} %constant.15.clone.near_ref), custom_call_target="tpu_custom_call" | custom-call | tf_op jit(solution)/shard_map/whiten/pallas_call | solution.py:174
  45.0 33.7 %all_to_all.15 = bf16[256,8,128]{2,1,0:T(8,128)(2,1)} all-to-all(bf16[256,8,128]{2,1,0:T(8,128)(2,1)} %bitcast.9), channel_id=1, replica_groups=mesh['chan'=16,'win'=16] {'chan','win'}, dimensions={0} | all-to-all | bytes 1048576 | tf_op jit(solution)/shard_map/all_to_all | solution.py:190
  78.8 2.8 %cross.1 = f32[512,128]{1,0:T(8,128)} custom-call(bf16[2048,128]{1,0:T(8,128)(2,1)} %bitcast.8), custom_call_target="tpu_custom_call" | custom-call | tf_op jit(solution)/shard_map/cross/pallas_call | solution.py:191
  81.6 23.0 %all_to_all.16 = f32[256,2,128]{2,1,0:T(2,128)} all-to-all(f32[256,2,128]{2,1,0:T(2,128)} %bitcast.11), channel_id=1, replica_groups=mesh['chan'=16,'win'=16] {'chan','win'}, dimensions={0} | all-to-all | bytes 524288 | tf_op jit(solution)/shard_map/all_to_all | solution.py:196
  104.6 4.2 %lag.1 = bf16[64,1024]{1,0:T(8,128)(2,1)} custom-call(f32[512,128]{1,0:T(8,128)} %bitcast.10, bf16[1024,1024]{1,0:T(8,128)(2,1)} %constant.16.clone.hi_ref, bf16[1024,1024]{1,0:T(8,128)(2,1)} %constant.17.clone.lo_ref), custom_call_target="tpu_custom_call" | custom-call | tf_op jit(solution)/shard_map/lag/pallas_call | solution.py:197
Async XLA Ops:
  0.0 10.2 %copy-start = (f32[64]{0:T(128)S(1)}, f32[64]{0:T(128)}, u32[]{:S(2)}) copy-start(f32[64]{0:T(128)} %param.9) | copy-start | bytes 772
  0.0 35.5 %all-to-all-start = ((bf16[32,128,128]{2,1,0:T(8,128)(2,1)}), bf16[32,128,128]{2,1,0:T(8,128)(2,1)S(1)}, u32[]{:S(2)}, u32[]{:S(2)}) async-start(bf16[32,128,128]{2,1,0:T(8,128)(2,1)} %param.8), calls=%async_computation | async-start | bytes 2097152 | tf_op jit(solution)/shard_map/all_to_all | solution.py:163
  35.5 1.0 copy-start.1

commit v2 on v1

v2 whole, which is shorter than its diff:
```python
import functools
import math

import jax
import jax.numpy as jnp
import ml_dtypes
import numpy as np
from jax import lax
from jax.experimental import pallas as pl
from jax.experimental.pallas import tpu as pltpu
from jax.sharding import PartitionSpec as P

LENGTH = 2048
BAND = 512
FIRST_BIN = 16
LAGS = 512
HALF_WIDTH = 32
TAPS = 64
CHANNELS = 128
WINDOWS = 512
BOTH = ("chan", "win")
RADIX = 4
QUARTER = LENGTH // RADIX
PER_CLASS = BAND // RADIX

BF16 = jnp.bfloat16
F32 = jnp.float32


def split_table(table):
    hi = table.astype(ml_dtypes.bfloat16)
    lo = (table - hi.astype(np.float64)).astype(ml_dtypes.bfloat16)
    return hi, lo


def phases(rows, cols):
    return 2.0 * math.pi / LENGTH * np.mod(rows[:, None] * cols[None, :], LENGTH).astype(np.float64)


@functools.cache
def tables():
    order = (RADIX * np.arange(PER_CLASS)[None, :] + np.arange(RADIX)[:, None]).reshape(-1)
    bins = FIRST_BIN + order
    cos, sin = (f(phases(bins, np.arange(QUARTER))).reshape(RADIX, PER_CLASS, QUARTER) for f in (np.cos, np.sin))
    even = [np.concatenate([cos[r], -sin[r]]) for r in (0, 2)]
    odd = np.concatenate(
        [
            np.concatenate([np.concatenate([cos[r], -s * sin[r]], axis=1), np.concatenate([-sin[r], -s * cos[r]], axis=1)])
            for r, s in ((1, 1), (3, -1))
        ]
    )
    forward = [np.concatenate(split_table(t)) for t in (*even, odd)]
    offset = np.mod(order[:, None] - order[None, :], BAND)
    near = (offset <= HALF_WIDTH) | (offset >= BAND - HALF_WIDTH)
    angles = phases(bins, np.arange(TAPS))
    taps = np.concatenate([np.cos(angles), -np.sin(angles)]).astype(np.float32)
    owned = order.reshape(2, 2, PER_CLASS).transpose(1, 0, 2).reshape(-1)
    angles = phases(FIRST_BIN + owned, np.arange(2 * LAGS) - LAGS)
    inverse = np.stack([np.cos(angles), -np.sin(angles)], axis=1) / (WINDOWS * BAND)
    return forward, near.astype(ml_dtypes.bfloat16), split_table(inverse.reshape(2 * BAND, 2 * LAGS)), taps


def dot_nt(a, b):
    return lax.dot_general(a, b, (((1,), (1,)), ((), ())), preferred_element_type=F32)


def dot_tn(a, b):
    return lax.dot_general(a, b, (((0,), (0,)), ((), ())), preferred_element_type=F32)


def dot_nn(a, b):
    return jnp.dot(a, b, preferred_element_type=F32)


def two_terms(x):
    hi = x.astype(BF16)
    return hi, (x - hi.astype(F32)).astype(BF16)


def swap_halves(low, high, bit, shift, axis):
    size = low.shape[axis]
    new_low = jnp.where(bit, pltpu.roll(high, shift, axis), low)
    new_high = jnp.where(bit, high, pltpu.roll(low, size - shift, axis))
    return new_low, new_high


def whiten_kernel(
    y_ref, odd_ref, even_hbm, half_hbm, near_hbm, resp_hbm, out_ref, even_ref, half_ref, near_ref, resp_ref, sems
):
    pairs = ((even_hbm, even_ref), (half_hbm, half_ref), (resp_hbm, resp_ref), (near_hbm, near_ref))
    copies = [pltpu.make_async_copy(src, dst, sems.at[k]) for k, (src, dst) in enumerate(pairs)]
    for copy in copies:
        copy.start()
    blocks = y_ref.shape[0] // RADIX
    sums = [[], [], [], []]
    for j in range(blocks):
        u = [y_ref[h * blocks + j].astype(F32) for h in range(RADIX)]
        even, odd = u[0] + u[2], u[1] + u[3]
        for k, x in enumerate((even + odd, even - odd, u[0] - u[2], u[1] - u[3])):
            sums[k].append(two_terms(x))
    terms = [[jnp.concatenate([x[t] for x in s], axis=1) for t in range(2)] for s in sums]
    inputs = [terms[0], terms[1], [jnp.concatenate([terms[2][t], terms[3][t]], axis=1) for t in range(2)]]
    spec = []
    for k, ref in enumerate((even_ref, half_ref, odd_ref)):
        hi, lo = inputs[k]
        rows = ref.shape[0] // 2
        if k < 2:
            copies[k].wait()
        both = dot_nt(ref[...], hi)
        spec.append(both[:rows] + both[rows:] + dot_nt(ref[:rows], lo))
    copies[2].wait()
    copies[3].wait()
    m = PER_CLASS
    spec_re = jnp.concatenate([spec[0][:m], spec[2][:m], spec[1][:m], spec[2][2 * m : 3 * m]])
    spec_im = jnp.concatenate([spec[0][m:], spec[2][m : 2 * m], spec[1][m:], spec[2][3 * m :]])
    resp_re = jnp.concatenate([resp_ref[:BAND]] * 2, axis=1)
    resp_im = jnp.concatenate([resp_ref[BAND:]] * 2, axis=1)
    filt_re = spec_re * resp_re - spec_im * resp_im
    filt_im = spec_re * resp_im + spec_im * resp_re
    power = filt_re * filt_re + filt_im * filt_im
    first = power.astype(BF16)
    second, third = two_terms(power - first.astype(F32))
    near = near_ref[...]
    smooth = (dot_nn(near, first) + dot_nn(near, second) + dot_nn(near, third)) * (1.0 / (2 * HALF_WIDTH + 1))
    inv_amp = lax.rsqrt(smooth + 1e-06)
    white = (filt_re * inv_amp, filt_im * inv_amp)
    row = lax.broadcasted_iota(jnp.int32, (m, CHANNELS), 0)
    bits = [(row & s) != 0 for s in (4, 2, 1)]
    for high in range(2):
        a = []
        for k in range(8):
            r = 2 * high + k // 4
            w = k % 2
            a.append(white[k // 2 % 2][r * m : (r + 1) * m, w * CHANNELS : (w + 1) * CHANNELS])
        for bit, shift in zip(bits, (4, 2, 1)):
            for k in range(8):
                if not k & shift:
                    a[k], a[k | shift] = swap_halves(a[k], a[k | shift], bit, shift, 0)
        for k in range(8):
            out_ref[high, :, k] = a[k].reshape(m // 8, 8, CHANNELS).astype(BF16)


def cross_kernel(b_ref, out_ref):
    wide = b_ref[...].astype(F32)
    first, second = wide[:, :8], wide[:, 8:]
    bit = (lax.broadcasted_iota(jnp.int32, first.shape, 1) & 4) != 0
    imag = (lax.broadcasted_iota(jnp.int32, first.shape, 1) & 2) != 0
    parts = []
    for x in swap_halves(first, second, bit, 4, 1):
        turned = jnp.where(imag, pltpu.roll(x, 2, 1), -pltpu.roll(x, 6, 1))
        x, turned = (v.astype(BF16).reshape(-1, CHANNELS) for v in (x, turned))
        cross = dot_tn(x, jnp.concatenate([x, turned], axis=1))
        parts.append([cross[:, :CHANNELS], cross[:, CHANNELS:]])
    row = lax.broadcasted_iota(jnp.int32, (CHANNELS, CHANNELS), 0)
    lane = lax.broadcasted_iota(jnp.int32, (CHANNELS, CHANNELS), 1)
    for down, right in ((4, 32), (2, 16), (1, 8)):
        row_bit = (row & down) != 0
        lane_bit = (lane & right) != 0
        for f in range(2):
            for part in range(2):
                a = parts[f][part]
                up = pltpu.roll(pltpu.roll(a, CHANNELS - down, 0), right, 1)
                dn = pltpu.roll(pltpu.roll(a, down, 0), CHANNELS - right, 1)
                parts[f][part] = jnp.where(row_bit == lane_bit, a, jnp.where(row_bit, dn, up))
    lane_bit = (lane & 64) != 0
    for part in range(2):
        for high, a in enumerate(swap_halves(parts[0][part], parts[1][part], lane_bit, 64, 1)):
            for c in range(CHANNELS // 8):
                start = c * 32 + high * 16 + part
                out_ref[pl.ds(start, 8, stride=2), :] = a[c * 8 : c * 8 + 8]


def lag_kernel(c_ref, hi_ref, lo_ref, out_ref):
    turned = c_ref[...].T
    hi, lo = two_terms(jnp.concatenate([turned[:64], turned[64:]], axis=1))
    both = dot_nn(jnp.concatenate([hi, lo], axis=0), hi_ref[...])
    total = both[:64] + (both[64:] + dot_nn(hi, lo_ref[...]))
    out_ref[...] = total.astype(BF16)


def kernel_call(kernel, out_shape, name, args, in_hbm=(), scratch=(), limit=24):
    vmem, hbm = pl.BlockSpec(memory_space=pltpu.VMEM), pl.BlockSpec(memory_space=pl.ANY)
    return pl.pallas_call(
        kernel,
        in_specs=[hbm if k in in_hbm else vmem for k in range(len(args))],
        out_specs=vmem,
        out_shape=out_shape,
        scratch_shapes=scratch,
        name=name,
        compiler_params=pltpu.CompilerParams(vmem_limit_bytes=limit << 20),
    )(*[pltpu.with_memory_space_constraint(a, pltpu.HBM if k in in_hbm else pltpu.VMEM) for k, a in enumerate(args)])


def body(records, fir_taps):
    forward, near, (inv_hi, inv_lo), taps_table = tables()
    y = lax.all_to_all(records, "chan", 0, 0, tiled=True)
    y = y.reshape(LENGTH // CHANNELS, 2 * CHANNELS, CHANNELS)
    response = jnp.dot(
        taps_table,
        jnp.broadcast_to(fir_taps[:, None], (TAPS, 128)),
        precision=lax.Precision.HIGHEST,
        preferred_element_type=F32,
    )
    even, half, odd = forward
    staged = (even, half, near, response)
    white = kernel_call(
        whiten_kernel,
        pltpu.VMEM((2, PER_CLASS // 8, 8, 8, CHANNELS), BF16),
        "whiten",
        (y, odd, *staged),
        in_hbm=(2, 3, 4, 5),
        scratch=[*(pltpu.VMEM(t.shape, t.dtype) for t in staged), pltpu.SemaphoreType.DMA((len(staged),))],
    )
    owners = BAND // 2
    white = lax.all_to_all(white.reshape(owners, 8, CHANNELS), BOTH, 0, 0, tiled=True)
    cross = kernel_call(
        cross_kernel,
        pltpu.VMEM((2 * owners, 128), F32),
        "cross",
        (white.reshape(owners // 2, 16, CHANNELS),),
    )
    cross = lax.all_to_all(cross.reshape(owners, 2, 128), BOTH, 0, 0, tiled=True)
    lagged = kernel_call(
        lag_kernel,
        jax.ShapeDtypeStruct((64, 2 * LAGS), BF16),
        "lag",
        (cross.reshape(2 * owners, 128), inv_hi, inv_lo),
    )
    return lagged.reshape(8, 8, 2 * LAGS)


def solution(mesh):
    in_specs = (P("win", None, "chan"), P())
    out_specs = P("chan", "win", None)
    return jax.shard_map(body, mesh=mesh, in_specs=in_specs, out_specs=out_specs, check_vma=False)
```

time: 109 us -> 97.9 us (0.90)
  Pallas kernels: 15.6 us -> 7.23 us
  blocking collectives: 56.7 us -> 54.9 us
    pallas_call x3, Pallas kernels: 15.6 us -> 7.23 us  [kernel_call(): pl.pallas_call(kernel, in_specs=[hbm if k in in_hbm else vmem for k in ra...]
    all_to_all x1, blocking collectives: 23 us -> 21.4 us  [body(): lax.all_to_all(cross.reshape(owners, 2, 128), BOTH, 0, 0, tiled=True)]
  transfers between devices with their start and end apart: 1 -> 1, of which waited for: 1 -> 1; matrix products, arithmetic and copies ran while one was open for 2% -> 3% of each run, Pallas kernels for 0% -> 0%
where the time goes in v2:
time: 97.9 us; the launch traced here: 97.6 us
  blocking collectives  54.9 us (56%)
  waiting for transfers between devices  22.8 us (23%)
  starting transfers between devices  10.2 us (10%)
  Pallas kernels  7.23 us (7%)
  matrix products  2.46 us (3%)
    all_to_all x1, blocking collectives, body(): lax.all_to_all(white.reshape(owners, 8, CHANNELS), BOTH, 0, 0, tiled=True)  33.4 us
    all_to_all x1, waiting for transfers between devices, body(): y = lax.all_to_all(records, 'chan', 0, 0, tiled=True)  22.8 us
    all_to_all x1, blocking collectives, body(): lax.all_to_all(cross.reshape(owners, 2, 128), BOTH, 0, 0, tiled=True)  21.4 us
    all_to_all x1, starting transfers between devices, body(): y = lax.all_to_all(records, 'chan', 0, 0, tiled=True)  10.2 us
    pallas_call x3, Pallas kernels, kernel_call(): pl.pallas_call(kernel, in_specs=[hbm if k in in_hbm else vmem for k in ra...  7.23 us
    dot_general x1, matrix products, body(): jnp.dot(taps_table, jnp.broadcast_to(fir_taps[:, None], (TAPS, 128)), pre...  2.46 us
  transfers between devices with their start and end apart: 1, of which 1 were waited for; matrix products, arithmetic and copies ran while one was open for 3% of the time, Pallas kernels for 0%

profile of v2, /device:TPU:1, one launch (start us, length us, event | category | flops | bytes accessed | tf_op | source)
XLA Modules:
  0.0 97.6 jit_solution(7525786547576231896)
XLA Ops:
  0.0 0.0 copy-start
  0.0 0.0 copy-start.3
  0.0 10.2 %all-to-all-start = ((bf16[32,128,128]{2,1,0:T(8,128)(2,1)}), bf16[32,128,128]{2,1,0:T(8,128)(2,1)S(1)}, u32[]{:S(2)}, u32[]{:S(2)}) async-start(bf16[32,128,128]{2,1,0:T(8,128)(2,1)} %param.9), calls=%async_computation | async-start | bytes 2097152 | tf_op jit(solution)/shard_map/all_to_all | solution.py:196
  10.2 0.0 copy-done
  10.2 2.5 %fusion.resp_hbm = f32[1024,128]{1,0:T(8,128)} fusion(f32[1024,64]{1,0:T(8,128)} %constant.14.clone, f32[64]{0:T(128)S(1)} %copy-done), kind=kOutput, calls=%fused_computation | convolution fusion | flops 100663296 | bytes 786688 | tf_op jit(solution)/shard_map/dot_general | solution.py:198
  12.7 22.8 %all-to-all-done = bf16[32,128,128]{2,1,0:T(8,128)(2,1)S(1)} async-done(((bf16[32,128,128]{2,1,0:T(8,128)(2,1)}), bf16[32,128,128]{2,1,0:T(8,128)(2,1)S(1)}, u32[]{:S(2)}, u32[]{:S(2)}) %all-to-all-start) | async-done | bytes 1048608 | tf_op jit(solution)/shard_map/all_to_all | solution.py:196
  35.5 0.0 copy-done.3
  35.5 0.0 copy-start.2
  35.5 4.7 %whiten.1 = bf16[2,16,8,8,128]{4,3,2,1,0:T(8,128)(2,1)S(1)} custom-call(bf16[16,256,128]{2,1,0:T(8,128)(2,1)S(1)} %bitcast.7, bf16[1024,1024]{1,0:T(8,128)(2,1)S(1)} %copy-done.3, bf16[512,512]{1,0:T(8,128)(2,1)} %constant.16.clone.even_hbm, bf16[512,512]{1,0:T(8,128)(2,1)} %constant.17.clone.half_hbm, bf16[512,512]{1,0:T(8,128)(2,1)} %constant.18.clone.near_hbm, ...), custom_call_target="tpu_custom_call" | custom-call | tf_op jit(solution)/shard_map/whiten/pallas_call | solution.py:183
  40.2 0.0 copy-start.1
  40.2 33.4 %all_to_all.15 = bf16[256,8,128]{2,1,0:T(8,128)(2,1)S(1)} all-to-all(bf16[256,8,128]{2,1,0:T(8,128)(2,1)S(1)} %bitcast.9), channel_id=1, replica_groups=mesh['chan'=16,'win'=16] {'chan','win'}, dimensions={0} | all-to-all | bytes 1048576 | tf_op jit(solution)/shard_map/all_to_all | solution.py:215
  73.7 1.0 %cross.1 = f32[512,128]{1,0:T(8,128)S(1)} custom-call(bf16[128,16,128]{2,1,0:T(8,128)(2,1)S(1)} %bitcast.8), custom_call_target="tpu_custom_call" | custom-call | tf_op jit(solution)/shard_map/cross/pallas_call | solution.py:183
  74.7 21.4 %all_to_all.16 = f32[256,2,128]{2,1,0:T(2,128)S(1)} all-to-all(f32[256,2,128]{2,1,0:T(2,128)S(1)} %bitcast.11), channel_id=1, replica_groups=mesh['chan'=16,'win'=16] {'chan','win'}, dimensions={0} | all-to-all | bytes 524288 | tf_op jit(solution)/shard_map/all_to_all | solution.py:222
  96.1 0.0 copy-done.2
  96.1 0.0 copy-done.1
  96.1 1.5 %lag.1 = bf16[64,1024]{1,0:T(8,128)(2,1)} custom-call(f32[512,128]{1,0:T(8,128)S(1)} %bitcast.10, bf16[1024,1024]{1,0:T(8,128)(2,1)S(1)} %copy-done.2, bf16[1024,1024]{1,0:T(8,128)(2,1)S(1)} %copy-done.1), custom_call_target="tpu_custom_call" | custom-call | tf_op jit(solution)/shard_map/lag/pallas_call | solution.py:183
Async XLA Ops:
  0.0 10.2 %copy-start = (f32[64]{0:T(128)S(1)}, f32[64]{0:T(128)}, u32[]{:S(2)}) copy-start(f32[64]{0:T(128)} %param.10) | copy-start | bytes 772
  0.0 35.5 %copy-start.3 = (bf16[1024,1024]{1,0:T(8,128)(2,1)S(1)}, bf16[1024,1024]{1,0:T(8,128)(2,1)}, u32[]{:S(2)}) copy-start(bf16[1024,1024]{1,0:T(8,128)(2,1)} %constant.15.clone.odd_ref) | copy-start | bytes 6291460
  0.0 35.5 %all-to-all-start = ((bf16[32,128,128]{2,1,0:T(8,128)(2,1)}), bf16[32,128,128]{2,1,0:T(8,128)(2,1)S(1)}, u32[]{:S(2)}, u32[]{:S(2)}) async-start(bf16[32,128,128]{2,1,0:T(8,128)(2,1)} %param.9), calls=%async_computation | async-start | bytes 2097152 | tf_op jit(solution)/shard_map/all_to_all | solution.py:196
  35.5 60.6 %copy-start.2 = (bf16[1024,1024]{1,0:T(8,128)(2,1)S(1)}, bf16[1024,1024]{1,0:T(8,128)(2,1)}, u32[]{:S(2)}) copy-start(bf16[1024,1024]{1,0:T(8,128)(2,1)} %constant.19.clone.hi_ref) | copy-start | bytes 6291460
  40.2 55.9 %copy-start.1 = (bf16[1024,1024]{1,0:T(8,128)(2,1)S(1)}, bf16[1024,1024]{1,0:T(8,128)(2,1)}, u32[]{:S(2)}) copy-start(bf16[1024,1024]{1,0:T(8,128)(2,1)} %constant.20.clone.lo_ref) | copy-start | bytes 6291460

commit v3 on v2

--- a/solution.py
+++ b/solution.py
@@ -54,10 +54,10 @@
     near = (offset <= HALF_WIDTH) | (offset >= BAND - HALF_WIDTH)
     angles = phases(bins, np.arange(TAPS))
     taps = np.concatenate([np.cos(angles), -np.sin(angles)]).astype(np.float32)
-    owned = order.reshape(2, 2, PER_CLASS).transpose(1, 0, 2).reshape(-1)
+    owned = order.reshape(2, 2, PER_CLASS).transpose(1, 2, 0).reshape(-1)
     angles = phases(FIRST_BIN + owned, np.arange(2 * LAGS) - LAGS)
     inverse = np.stack([np.cos(angles), -np.sin(angles)], axis=1) / (WINDOWS * BAND)
-    return forward, near.astype(ml_dtypes.bfloat16), split_table(inverse.reshape(2 * BAND, 2 * LAGS)), taps
+    return forward, near.astype(ml_dtypes.bfloat16), np.concatenate(split_table(inverse.reshape(2 * BAND, 2 * LAGS))), taps
 
 
 def dot_nt(a, b):
@@ -137,62 +137,70 @@
                 if not k & shift:
                     a[k], a[k | shift] = swap_halves(a[k], a[k | shift], bit, shift, 0)
         for k in range(8):
-            out_ref[high, :, k] = a[k].reshape(m // 8, 8, CHANNELS).astype(BF16)
-
-
-def cross_kernel(b_ref, out_ref):
-    wide = b_ref[...].astype(F32)
-    first, second = wide[:, :8], wide[:, 8:]
-    bit = (lax.broadcasted_iota(jnp.int32, first.shape, 1) & 4) != 0
-    imag = (lax.broadcasted_iota(jnp.int32, first.shape, 1) & 2) != 0
-    parts = []
-    for x in swap_halves(first, second, bit, 4, 1):
-        turned = jnp.where(imag, pltpu.roll(x, 2, 1), -pltpu.roll(x, 6, 1))
-        x, turned = (v.astype(BF16).reshape(-1, CHANNELS) for v in (x, turned))
-        cross = dot_tn(x, jnp.concatenate([x, turned], axis=1))
-        parts.append([cross[:, :CHANNELS], cross[:, CHANNELS:]])
+            out_ref[:, k, high] = a[k].reshape(m // 8, 8, CHANNELS).astype(BF16)
+
+
+def cross_kernel(core_ref, own_ref, other_ref, out_ref):
+    core = core_ref[0]
     row = lax.broadcasted_iota(jnp.int32, (CHANNELS, CHANNELS), 0)
     lane = lax.broadcasted_iota(jnp.int32, (CHANNELS, CHANNELS), 1)
-    for down, right in ((4, 32), (2, 16), (1, 8)):
-        row_bit = (row & down) != 0
-        lane_bit = (lane & right) != 0
-        for f in range(2):
-            for part in range(2):
-                a = parts[f][part]
+    odd_block = (lane & 8) != 0
+    for high in range(2):
+        own, other = (ref[:, high * 8 : high * 8 + 8].astype(F32) for ref in (own_ref, other_ref))
+        bit = (lax.broadcasted_iota(jnp.int32, own.shape, 1) & 4) != 0
+        imag = (lax.broadcasted_iota(jnp.int32, own.shape, 1) & 2) != 0
+        parts = []
+        for x in swap_halves(own, other, bit, 4, 1):
+            turned = jnp.where(imag, pltpu.roll(x, 2, 1), -pltpu.roll(x, 6, 1))
+            x, turned = (v.astype(BF16).reshape(-1, CHANNELS) for v in (x, turned))
+            cross = dot_tn(x, jnp.concatenate([x, turned], axis=1))
+            parts.append([cross[:, :CHANNELS], cross[:, CHANNELS:]])
+        for part in range(2):
+            even, odd = swap_halves(parts[0][part], parts[1][part], odd_block, 8, 1)
+            a = jnp.where(core == 0, even, odd)
+            for down, right in ((4, 64), (2, 32), (1, 16)):
+                row_bit = (row & down) != 0
+                lane_bit = (lane & right) != 0
                 up = pltpu.roll(pltpu.roll(a, CHANNELS - down, 0), right, 1)
                 dn = pltpu.roll(pltpu.roll(a, down, 0), CHANNELS - right, 1)
-                parts[f][part] = jnp.where(row_bit == lane_bit, a, jnp.where(row_bit, dn, up))
-    lane_bit = (lane & 64) != 0
-    for part in range(2):
-        for high, a in enumerate(swap_halves(parts[0][part], parts[1][part], lane_bit, 64, 1)):
-            for c in range(CHANNELS // 8):
-                start = c * 32 + high * 16 + part
-                out_ref[pl.ds(start, 8, stride=2), :] = a[c * 8 : c * 8 + 8]
-
-
-def lag_kernel(c_ref, hi_ref, lo_ref, out_ref):
-    turned = c_ref[...].T
-    hi, lo = two_terms(jnp.concatenate([turned[:64], turned[64:]], axis=1))
-    both = dot_nn(jnp.concatenate([hi, lo], axis=0), hi_ref[...])
-    total = both[:64] + (both[64:] + dot_nn(hi, lo_ref[...]))
+                a = jnp.where(row_bit == lane_bit, a, jnp.where(row_bit, dn, up))
+            out_ref[pl.ds(2 * high + part, CHANNELS, stride=4), :] = a
+
+
+def lag_kernel(c_ref, table_ref, out_ref):
+    turned = c_ref[...].T.reshape(8, 2, 8, 4 * CHANNELS)
+    hi, lo = two_terms(jnp.concatenate([turned[:, f].reshape(64, 4 * CHANNELS) for f in range(2)], axis=1))
+    both = dot_nn(jnp.concatenate([hi, lo], axis=0), table_ref[: 2 * BAND])
+    total = both[:64] + (both[64:] + dot_nn(hi, table_ref[2 * BAND :]))
     out_ref[...] = total.astype(BF16)
 
 
-def kernel_call(kernel, out_shape, name, args, in_hbm=(), scratch=(), limit=24):
-    vmem, hbm = pl.BlockSpec(memory_space=pltpu.VMEM), pl.BlockSpec(memory_space=pl.ANY)
+def kernel_call(kernel, out_shape, name, args, in_hbm=(), in_smem=(), scratch=(), cost=None, limit=24):
+    specs, operands = [], []
+    for k, a in enumerate(args):
+        if k in in_smem:
+            specs.append(pl.BlockSpec(memory_space=pltpu.SMEM))
+        elif k in in_hbm:
+            specs.append(pl.BlockSpec(memory_space=pl.ANY))
+            a = pltpu.with_memory_space_constraint(a, pltpu.HBM)
+        else:
+            specs.append(pl.BlockSpec(memory_space=pltpu.VMEM))
+            a = pltpu.with_memory_space_constraint(a, pltpu.VMEM)
+        operands.append(a)
     return pl.pallas_call(
         kernel,
-        in_specs=[hbm if k in in_hbm else vmem for k in range(len(args))],
-        out_specs=vmem,
+        in_specs=specs,
+        out_specs=pl.BlockSpec(memory_space=pltpu.VMEM),
         out_shape=out_shape,
         scratch_shapes=scratch,
         name=name,
+        cost_estimate=cost,
         compiler_params=pltpu.CompilerParams(vmem_limit_bytes=limit << 20),
-    )(*[pltpu.with_memory_space_constraint(a, pltpu.HBM if k in in_hbm else pltpu.VMEM) for k, a in enumerate(args)])
+    )(*operands)
 
 
 def body(records, fir_taps):
-    forward, near, (inv_hi, inv_lo), taps_table = tables()
+    forward, near, inverse, taps_table = tables()
     y = lax.all_to_all(records, "chan", 0, 0, tiled=True)
     y = y.reshape(LENGTH // CHANNELS, 2 * CHANNELS, CHANNELS)
     response = jnp.dot(
@@ -205,26 +213,32 @@
     staged = (even, half, near, response)
     white = kernel_call(
         whiten_kernel,
-        pltpu.VMEM((2, PER_CLASS // 8, 8, 8, CHANNELS), BF16),
+        pltpu.VMEM((PER_CLASS // 8, 8, 2, 8, CHANNELS), BF16),
         "whiten",
         (y, odd, *staged),
         in_hbm=(2, 3, 4, 5),
         scratch=[*(pltpu.VMEM(t.shape, t.dtype) for t in staged), pltpu.SemaphoreType.DMA((len(staged),))],
     )
-    owners = BAND // 2
-    white = lax.all_to_all(white.reshape(owners, 8, CHANNELS), BOTH, 0, 0, tiled=True)
+    owners = PER_CLASS
+    groups = [list(range(core, 2 * owners, 2)) for core in range(2)]
+    white = white.reshape(owners, 16, CHANNELS)
+    white = lax.all_to_all(white, BOTH, 0, 0, tiled=True, axis_index_groups=groups)
+    other = lax.ppermute(white, BOTH, [(d, d ^ 1) for d in range(2 * owners)])
+    core = lax.rem(lax.axis_index("win"), 2).astype(jnp.int32).reshape(1)
     cross = kernel_call(
         cross_kernel,
-        pltpu.VMEM((2 * owners, 128), F32),
+        pltpu.VMEM((4 * owners, 128), F32),
         "cross",
-        (white.reshape(owners // 2, 16, CHANNELS),),
-    )
-    cross = lax.all_to_all(cross.reshape(owners, 2, 128), BOTH, 0, 0, tiled=True)
+        (core, white, other),
+        in_smem=(0,),
+        cost=pl.CostEstimate(flops=2 * 10**9, transcendentals=0, bytes_accessed=4 * 10**6),
+    )
+    cross = lax.all_to_all(cross.reshape(owners, 4, 128), BOTH, 0, 0, tiled=True, axis_index_groups=groups)
     lagged = kernel_call(
         lag_kernel,
         jax.ShapeDtypeStruct((64, 2 * LAGS), BF16),
         "lag",
-        (cross.reshape(2 * owners, 128), inv_hi, inv_lo),
+        (cross.reshape(4 * owners, 128), inverse),
     )
     return lagged.reshape(8, 8, 2 * LAGS)
 

time: 97.9 us -> 98 us (level)
  blocking collectives: 54.9 us -> 49.6 us
  starting transfers between devices: 10.2 us -> 12.9 us
  waiting for transfers between devices: 22.8 us -> 24.4 us
    all_to_all x2, blocking collectives: 54.9 us -> 49.6 us  [the longest x1 30.5 us: body(): lax.all_to_all(white, BOTH, 0, 0, tiled=True, axis_index_groups=groups)]
    ppermute x0 -> x1, starting transfers between devices: none -> 2.69 us  [body(): other = lax.ppermute(white, BOTH, [(d, d ^ 1) for d in range(2 * owners)])]
    ppermute x0 -> x1, waiting for transfers between devices: none -> 1.53 us  [body(): other = lax.ppermute(white, BOTH, [(d, d ^ 1) for d in range(2 * owners)])]
  transfers between devices with their start and end apart: 1 -> 2, of which waited for: 1 -> 2; matrix products, arithmetic and copies ran while one was open for 3% -> 3% of each run, Pallas kernels for 0% -> 0%
where the time goes in v3:
time: 98 us; the launch traced here: 97.2 us
  blocking collectives  49.6 us (51%)
  waiting for transfers between devices  24.4 us (25%)
  starting transfers between devices  12.9 us (13%)
  Pallas kernels  7.82 us (8%)
  matrix products  2.46 us (3%)
    all_to_all x1, blocking collectives, body(): lax.all_to_all(white, BOTH, 0, 0, tiled=True, axis_index_groups=groups)  30.5 us
    all_to_all x1, waiting for transfers between devices, body(): y = lax.all_to_all(records, 'chan', 0, 0, tiled=True)  22.8 us
    all_to_all x1, blocking collectives, body(): lax.all_to_all(cross.reshape(owners, 4, 128), BOTH, 0, 0, tiled=True, axi...  19.1 us
    all_to_all x1, starting transfers between devices, body(): y = lax.all_to_all(records, 'chan', 0, 0, tiled=True)  10.2 us
    pallas_call x3, Pallas kernels, kernel_call(): pl.pallas_call(kernel, in_specs=specs, out_specs=pl.BlockSpec(memory_spac...  7.82 us
    ppermute x1, starting transfers between devices, body(): other = lax.ppermute(white, BOTH, [(d, d ^ 1) for d in range(2 * owners)])  2.69 us
    dot_general x1, matrix products, body(): jnp.dot(taps_table, jnp.broadcast_to(fir_taps[:, None], (TAPS, 128)), pre...  2.46 us
  transfers between devices with their start and end apart: 2, of which 2 were waited for; matrix products, arithmetic and copies ran while one was open for 3% of the time, Pallas kernels for 0%

profile of v3, /device:TPU:1, one launch (start us, length us, event | category | flops | bytes accessed | tf_op | source)
XLA Modules:
  0.0 97.2 jit_solution(17183723403934907632)
XLA Ops:
  0.0 0.0 copy-start
  0.0 0.0 copy-start.2
  0.0 10.2 %all-to-all-start = ((bf16[32,128,128]{2,1,0:T(8,128)(2,1)}), bf16[32,128,128]{2,1,0:T(8,128)(2,1)S(1)}, u32[]{:S(2)}, u32[]{:S(2)}) async-start(bf16[32,128,128]{2,1,0:T(8,128)(2,1)} %param.8), calls=%async_computation | async-start | bytes 2097152 | tf_op jit(solution)/shard_map/all_to_all | solution.py:204
  10.2 0.0 copy-done
  10.2 2.5 %fusion.resp_hbm = f32[1024,128]{1,0:T(8,128)} fusion(f32[1024,64]{1,0:T(8,128)} %constant.21.clone, f32[64]{0:T(128)S(1)} %copy-done), kind=kOutput, calls=%fused_computation | convolution fusion | flops 100663296 | bytes 786688 | tf_op jit(solution)/shard_map/dot_general | solution.py:206
  12.7 22.8 %all-to-all-done = bf16[32,128,128]{2,1,0:T(8,128)(2,1)S(1)} async-done(((bf16[32,128,128]{2,1,0:T(8,128)(2,1)}), bf16[32,128,128]{2,1,0:T(8,128)(2,1)S(1)}, u32[]{:S(2)}, u32[]{:S(2)}) %all-to-all-start) | async-done | bytes 1048608 | tf_op jit(solution)/shard_map/all_to_all | solution.py:204
  35.5 0.0 copy-done.2
  35.5 4.6 %whiten.1 = bf16[16,8,2,8,128]{4,3,2,1,0:T(8,128)(2,1)S(1)} custom-call(bf16[16,256,128]{2,1,0:T(8,128)(2,1)S(1)} %bitcast.7, bf16[1024,1024]{1,0:T(8,128)(2,1)S(1)} %copy-done.2, bf16[512,512]{1,0:T(8,128)(2,1)} %constant.23.clone.even_hbm, bf16[512,512]{1,0:T(8,128)(2,1)} %constant.24.clone.half_hbm, bf16[512,512]{1,0:T(8,128)(2,1)} %constant.25.clone.near_hbm, ...), custom_call_target="tpu_custom_call" | custom-call | tf_op jit(solution)/shard_map/whiten/pallas_call | solution.py:190
  40.1 30.5 %all_to_all.15.own_ref = bf16[128,16,128]{2,1,0:T(8,128)(2,1)S(1)} all-to-all(bf16[128,16,128]{2,1,0:T(8,128)(2,1)S(1)} %bitcast.8), channel_id=1, replica_groups={{0,2,4,6,8,10,12,14,16,18,20,22,24,26,28,30,32,34,36,38,40,42,44,46,48,..., dimensions={0} | all-to-all | bytes 1048576 | tf_op jit(solution)/shard_map/all_to_all | solution.py:225
  70.6 2.7 %collective-permute-start = (bf16[128,16,128]{2,1,0:T(8,128)(2,1)S(1)}, bf16[128,16,128]{2,1,0:T(8,128)(2,1)S(1)}, u32[]{:S(2)}, u32[]{:S(2)}) collective-permute-start(bf16[128,16,128]{2,1,0:T(8,128)(2,1)S(1)} %all_to_all.15.own_ref), channel_id=1, source_target_pairs={{0,1},{1,0},{2,3},{3,2},{4,5},{5,4},{6,7},{7,6},{8,9},{9,8},{10,11... | collective-permute-start | bytes 1572872 | tf_op jit(solution)/shard_map/ppermute | solution.py:226
  73.3 0.0 copy-start.1
  73.3 1.5 %collective-permute-done.other_ref = bf16[128,16,128]{2,1,0:T(8,128)(2,1)S(1)} collective-permute-done((bf16[128,16,128]{2,1,0:T(8,128)(2,1)S(1)}, bf16[128,16,128]{2,1,0:T(8,128)(2,1)S(1)}, u32[]{:S(2)}, u32[]{:S(2)}) %collective-permute-start) | collective-permute-done | bytes 524320 | tf_op jit(solution)/shard_map/ppermute | solution.py:226
  74.8 1.8 %cross.1 = f32[512,128]{1,0:T(8,128)S(1)} custom-call(s32[1]{0:T(128)} %bitcast.core_ref, bf16[128,16,128]{2,1,0:T(8,128)(2,1)S(1)} %all_to_all.15.own_ref, bf16[128,16,128]{2,1,0:T(8,128)(2,1)S(1)} %collective-permute-done.other_ref), custom_call_target="tpu_custom_call" | custom-call | flops 2000000000 | bytes 4000000 | tf_op jit(solution)/shard_map/cross/pallas_call | solution.py:190
  76.6 19.1 %all_to_all.16 = f32[128,4,128]{2,1,0:T(4,128)S(1)} all-to-all(f32[128,4,128]{2,1,0:T(4,128)S(1)} %bitcast.10), channel_id=1, replica_groups={{0,2,4,6,8,10,12,14,16,18,20,22,24,26,28,30,32,34,36,38,40,42,44,46,48,..., dimensions={0} | all-to-all | bytes 524288 | tf_op jit(solution)/shard_map/all_to_all | solution.py:236
  95.7 0.0 copy-done.1
  95.7 1.5 %lag.1 = bf16[64,1024]{1,0:T(8,128)(2,1)} custom-call(f32[512,128]{1,0:T(8,128)S(1)} %bitcast.9, bf16[2048,1024]{1,0:T(8,128)(2,1)S(1)} %copy-done.1), custom_call_target="tpu_custom_call" | custom-call | tf_op jit(solution)/shard_map/lag/pallas_call | solution.py:190
Async XLA Ops:
  0.0 10.2 %copy-start = (f32[64]{0:T(128)S(1)}, f32[64]{0:T(128)}, u32[]{:S(2)}) copy-start(f32[64]{0:T(128)} %param.9) | copy-start | bytes 772
  0.0 35.5 %copy-start.2 = (bf16[1024,1024]{1,0:T(8,128)(2,1)S(1)}, bf16[1024,1024]{1,0:T(8,128)(2,1)}, u32[]{:S(2)}) copy-start(bf16[1024,1024]{1,0:T(8,128)(2,1)} %constant.22.clone.odd_ref) | copy-start | bytes 6291460
  0.0 35.5 %all-to-all-start = ((bf16[32,128,128]{2,1,0:T(8,128)(2,1)}), bf16[32,128,128]{2,1,0:T(8,128)(2,1)S(1)}, u32[]{:S(2)}, u32[]{:S(2)}) async-start(bf16[32,128,128]{2,1,0:T(8,128)(2,1)} %param.8), calls=%async_computation | async-start | bytes 2097152 | tf_op jit(solution)/shard_map/all_to_all | solution.py:204
  70.6 4.2 %collective-permute-start = (bf16[128,16,128]{2,1,0:T(8,128)(2,1)S(1)}, bf16[128,16,128]{2,1,0:T(8,128)(2,1)S(1)}, u32[]{:S(2)}, u32[]{:S(2)}) collective-permute-start(bf16[128,16,128]{2,1,0:T(8,128)(2,1)S(1)} %all_to_all.15.own_ref), channel_id=1, source_target_pairs={{0,1},{1,0},{2,3},{3,2},{4,5},{5,4},{6,7},{7,6},{8,9},{9,8},{10,11... | collective-permute-start | bytes 1572872 | tf_op jit(solution)/shard_map/ppermute | solution.py:226
  73.3 22.4 %copy-start.1 = (bf16[2048,1024]{1,0:T(8,128)(2,1)S(1)}, bf16[2048,1024]{1,0:T(8,128)(2,1)}, u32[]{:S(2)}) copy-start(bf16[2048,1024]{1,0:T(8,128)(2,1)} %constant.26.clone.table_ref) | copy-start | bytes 12582916

commit v4 on v2

--- a/solution.py
+++ b/solution.py
@@ -18,7 +18,7 @@
 TAPS = 64
 CHANNELS = 128
 WINDOWS = 512
-BOTH = ("chan", "win")
+BOTH = ("win", "chan")
 RADIX = 4
 QUARTER = LENGTH // RADIX
 PER_CLASS = BAND // RADIX
@@ -100,14 +100,14 @@
             sums[k].append(two_terms(x))
     terms = [[jnp.concatenate([x[t] for x in s], axis=1) for t in range(2)] for s in sums]
     inputs = [terms[0], terms[1], [jnp.concatenate([terms[2][t], terms[3][t]], axis=1) for t in range(2)]]
-    spec = []
-    for k, ref in enumerate((even_ref, half_ref, odd_ref)):
+    spec = {}
+    for k, ref in ((2, odd_ref), (0, even_ref), (1, half_ref)):
         hi, lo = inputs[k]
         rows = ref.shape[0] // 2
         if k < 2:
             copies[k].wait()
         both = dot_nt(ref[...], hi)
-        spec.append(both[:rows] + both[rows:] + dot_nt(ref[:rows], lo))
+        spec[k] = both[:rows] + both[rows:] + dot_nt(ref[:rows], lo)
     copies[2].wait()
     copies[3].wait()
     m = PER_CLASS
@@ -118,10 +118,9 @@
     filt_re = spec_re * resp_re - spec_im * resp_im
     filt_im = spec_re * resp_im + spec_im * resp_re
     power = filt_re * filt_re + filt_im * filt_im
-    first = power.astype(BF16)
-    second, third = two_terms(power - first.astype(F32))
+    hi, lo = two_terms(power)
     near = near_ref[...]
-    smooth = (dot_nn(near, first) + dot_nn(near, second) + dot_nn(near, third)) * (1.0 / (2 * HALF_WIDTH + 1))
+    smooth = (dot_nn(near, hi) + dot_nn(near, lo)) * (1.0 / (2 * HALF_WIDTH + 1))
     inv_amp = lax.rsqrt(smooth + 1e-06)
     white = (filt_re * inv_amp, filt_im * inv_amp)
     row = lax.broadcasted_iota(jnp.int32, (m, CHANNELS), 0)
@@ -166,8 +165,8 @@
     for part in range(2):
         for high, a in enumerate(swap_halves(parts[0][part], parts[1][part], lane_bit, 64, 1)):
             for c in range(CHANNELS // 8):
-                start = c * 32 + high * 16 + part
-                out_ref[pl.ds(start, 8, stride=2), :] = a[c * 8 : c * 8 + 8]
+                start = high * 256 + c * 2 + part
+                out_ref[pl.ds(start, 8, stride=32), :] = a[c * 8 : c * 8 + 8]
 
 
 def lag_kernel(c_ref, hi_ref, lo_ref, out_ref):

time: 97.9 us -> 96.6 us (0.987)
  blocking collectives: 54.9 us -> 53.2 us
    all_to_all x1, blocking collectives: 21.4 us -> 20.2 us  [body(): lax.all_to_all(cross.reshape(owners, 2, 128), BOTH, 0, 0, tiled=True)]
where the time goes in v4:
time: 96.6 us; the launch traced here: 96.3 us
  blocking collectives  53.2 us (55%)
  waiting for transfers between devices  22.8 us (24%)
  starting transfers between devices  10.2 us (11%)
  Pallas kernels  7.53 us (8%)
  matrix products  2.46 us (3%)
    all_to_all x1, blocking collectives, body(): lax.all_to_all(white.reshape(owners, 8, CHANNELS), BOTH, 0, 0, tiled=True)  33 us
    all_to_all x1, waiting for transfers between devices, body(): y = lax.all_to_all(records, 'chan', 0, 0, tiled=True)  22.8 us
    all_to_all x1, blocking collectives, body(): lax.all_to_all(cross.reshape(owners, 2, 128), BOTH, 0, 0, tiled=True)  20.2 us
    all_to_all x1, starting transfers between devices, body(): y = lax.all_to_all(records, 'chan', 0, 0, tiled=True)  10.2 us
    pallas_call x3, Pallas kernels, kernel_call(): pl.pallas_call(kernel, in_specs=[hbm if k in in_hbm else vmem for k in ra...  7.53 us
    dot_general x1, matrix products, body(): jnp.dot(taps_table, jnp.broadcast_to(fir_taps[:, None], (TAPS, 128)), pre...  2.46 us
  transfers between devices with their start and end apart: 1, of which 1 were waited for; matrix products, arithmetic and copies ran while one was open for 3% of the time, Pallas kernels for 0%

profile of v4, /device:TPU:1, one launch (start us, length us, event | category | flops | bytes accessed | tf_op | source)
XLA Modules:
  0.0 96.3 jit_solution(929603162179591889)
XLA Ops:
  0.0 0.0 copy-start
  0.0 0.0 copy-start.3
  0.0 10.2 %all-to-all-start = ((bf16[32,128,128]{2,1,0:T(8,128)(2,1)}), bf16[32,128,128]{2,1,0:T(8,128)(2,1)S(1)}, u32[]{:S(2)}, u32[]{:S(2)}) async-start(bf16[32,128,128]{2,1,0:T(8,128)(2,1)} %param.9), calls=%async_computation | async-start | bytes 2097152 | tf_op jit(solution)/shard_map/all_to_all | solution.py:195
  10.2 0.0 copy-done
  10.2 2.5 %fusion.resp_hbm = f32[1024,128]{1,0:T(8,128)} fusion(f32[1024,64]{1,0:T(8,128)} %constant.14.clone, f32[64]{0:T(128)S(1)} %copy-done), kind=kOutput, calls=%fused_computation | convolution fusion | flops 100663296 | bytes 786688 | tf_op jit(solution)/shard_map/dot_general | solution.py:197
  12.7 22.8 %all-to-all-done = bf16[32,128,128]{2,1,0:T(8,128)(2,1)S(1)} async-done(((bf16[32,128,128]{2,1,0:T(8,128)(2,1)}), bf16[32,128,128]{2,1,0:T(8,128)(2,1)S(1)}, u32[]{:S(2)}, u32[]{:S(2)}) %all-to-all-start) | async-done | bytes 1048608 | tf_op jit(solution)/shard_map/all_to_all | solution.py:195
  35.5 0.0 copy-done.3
  35.5 0.0 copy-start.2
  35.5 4.9 %whiten.1 = bf16[2,16,8,8,128]{4,3,2,1,0:T(8,128)(2,1)S(1)} custom-call(bf16[16,256,128]{2,1,0:T(8,128)(2,1)S(1)} %bitcast.7, bf16[1024,1024]{1,0:T(8,128)(2,1)S(1)} %copy-done.3, bf16[512,512]{1,0:T(8,128)(2,1)} %constant.16.clone.even_hbm, bf16[512,512]{1,0:T(8,128)(2,1)} %constant.17.clone.half_hbm, bf16[512,512]{1,0:T(8,128)(2,1)} %constant.18.clone.near_hbm, ...), custom_call_target="tpu_custom_call" | custom-call | tf_op jit(solution)/shard_map/whiten/pallas_call | solution.py:182
  40.4 0.0 copy-start.1
  40.5 33.0 %all_to_all.15 = bf16[256,8,128]{2,1,0:T(8,128)(2,1)S(1)} all-to-all(bf16[256,8,128]{2,1,0:T(8,128)(2,1)S(1)} %bitcast.9), channel_id=1, replica_groups=mesh['chan'=16,'win'=16] {'win','chan'}, dimensions={0} | all-to-all | bytes 1048576 | tf_op jit(solution)/shard_map/all_to_all | solution.py:214
  73.5 1.1 %cross.1 = f32[512,128]{1,0:T(8,128)S(1)} custom-call(bf16[128,16,128]{2,1,0:T(8,128)(2,1)S(1)} %bitcast.8), custom_call_target="tpu_custom_call" | custom-call | tf_op jit(solution)/shard_map/cross/pallas_call | solution.py:182
  74.6 20.2 %all_to_all.16 = f32[256,2,128]{2,1,0:T(2,128)S(1)} all-to-all(f32[256,2,128]{2,1,0:T(2,128)S(1)} %bitcast.11), channel_id=1, replica_groups=mesh['chan'=16,'win'=16] {'win','chan'}, dimensions={0} | all-to-all | bytes 524288 | tf_op jit(solution)/shard_map/all_to_all | solution.py:221
  94.8 0.0 copy-done.2
  94.8 0.0 copy-done.1
  94.8 1.5 %lag.1 = bf16[64,1024]{1,0:T(8,128)(2,1)} custom-call(f32[512,128]{1,0:T(8,128)S(1)} %bitcast.10, bf16[1024,1024]{1,0:T(8,128)(2,1)S(1)} %copy-done.2, bf16[1024,1024]{1,0:T(8,128)(2,1)S(1)} %copy-done.1), custom_call_target="tpu_custom_call" | custom-call | tf_op jit(solution)/shard_map/lag/pallas_call | solution.py:182
Async XLA Ops:
  0.0 10.2 %copy-start = (f32[64]{0:T(128)S(1)}, f32[64]{0:T(128)}, u32[]{:S(2)}) copy-start(f32[64]{0:T(128)} %param.10) | copy-start | bytes 772
  0.0 35.5 %copy-start.3 = (bf16[1024,1024]{1,0:T(8,128)(2,1)S(1)}, bf16[1024,1024]{1,0:T(8,128)(2,1)}, u32[]{:S(2)}) copy-start(bf16[1024,1024]{1,0:T(8,128)(2,1)} %constant.15.clone.odd_ref) | copy-start | bytes 6291460
  0.0 35.5 %all-to-all-start = ((bf16[32,128,128]{2,1,0:T(8,128)(2,1)}), bf16[32,128,128]{2,1,0:T(8,128)(2,1)S(1)}, u32[]{:S(2)}, u32[]{:S(2)}) async-start(bf16[32,128,128]{2,1,0:T(8,128)(2,1)} %param.9), calls=%async_computation | async-start | bytes 2097152 | tf_op jit(solution)/shard_map/all_to_all | solution.py:195
  35.5 59.3 %copy-start.2 = (bf16[1024,1024]{1,0:T(8,128)(2,1)S(1)}, bf16[1024,1024]{1,0:T(8,128)(2,1)}, u32[]{:S(2)}) copy-start(bf16[1024,1024]{1,0:T(8,128)(2,1)} %constant.19.clone.hi_ref) | copy-start | bytes 6291460
  40.4 54.4 %copy-start.1 = (bf16[1024,1024]{1,0:T(8,128)(2,1)S(1)}, bf16[1024,1024]{1,0:T(8,128)(2,1)}, u32[]{:S(2)}) copy-start(bf16[1024,1024]{1,0:T(8,128)(2,1)} %constant.20.clone.lo_ref) | copy-start | bytes 6291460

commit v5 on v4

--- a/solution.py
+++ b/solution.py
@@ -85,12 +85,10 @@
 
 
 def whiten_kernel(
-    y_ref, odd_ref, even_hbm, half_hbm, near_hbm, resp_hbm, out_ref, even_ref, half_ref, near_ref, resp_ref, sems
+    y_ref, even_ref, half_ref, near_ref, resp_ref, odd_hbm, out_ref, odd_ref, sem
 ):
-    pairs = ((even_hbm, even_ref), (half_hbm, half_ref), (resp_hbm, resp_ref), (near_hbm, near_ref))
-    copies = [pltpu.make_async_copy(src, dst, sems.at[k]) for k, (src, dst) in enumerate(pairs)]
-    for copy in copies:
-        copy.start()
+    copy = pltpu.make_async_copy(odd_hbm, odd_ref, sem)
+    copy.start()
     blocks = y_ref.shape[0] // RADIX
     sums = [[], [], [], []]
     for j in range(blocks):
@@ -100,16 +98,14 @@
             sums[k].append(two_terms(x))
     terms = [[jnp.concatenate([x[t] for x in s], axis=1) for t in range(2)] for s in sums]
     inputs = [terms[0], terms[1], [jnp.concatenate([terms[2][t], terms[3][t]], axis=1) for t in range(2)]]
-    spec = {}
-    for k, ref in ((2, odd_ref), (0, even_ref), (1, half_ref)):
+    spec = [None] * 3
+    for k, ref in enumerate((even_ref, half_ref, odd_ref)):
         hi, lo = inputs[k]
         rows = ref.shape[0] // 2
-        if k < 2:
-            copies[k].wait()
+        if k == 2:
+            copy.wait()
         both = dot_nt(ref[...], hi)
         spec[k] = both[:rows] + both[rows:] + dot_nt(ref[:rows], lo)
-    copies[2].wait()
-    copies[3].wait()
     m = PER_CLASS
     spec_re = jnp.concatenate([spec[0][:m], spec[2][:m], spec[1][:m], spec[2][2 * m : 3 * m]])
     spec_im = jnp.concatenate([spec[0][m:], spec[2][m : 2 * m], spec[1][m:], spec[2][3 * m :]])
@@ -177,7 +173,7 @@
     out_ref[...] = total.astype(BF16)
 
 
-def kernel_call(kernel, out_shape, name, args, in_hbm=(), scratch=(), limit=24):
+def kernel_call(kernel, out_shape, name, args, in_hbm=(), scratch=(), cost=None, limit=24):
     vmem, hbm = pl.BlockSpec(memory_space=pltpu.VMEM), pl.BlockSpec(memory_space=pl.ANY)
     return pl.pallas_call(
         kernel,
@@ -186,6 +182,7 @@
         out_shape=out_shape,
         scratch_shapes=scratch,
         name=name,
+        cost_estimate=cost,
         compiler_params=pltpu.CompilerParams(vmem_limit_bytes=limit << 20),
     )(*[pltpu.with_memory_space_constraint(a, pltpu.HBM if k in in_hbm else pltpu.VMEM) for k, a in enumerate(args)])
 
@@ -201,14 +198,13 @@
         preferred_element_type=F32,
     )
     even, half, odd = forward
-    staged = (even, half, near, response)
     white = kernel_call(
         whiten_kernel,
         pltpu.VMEM((2, PER_CLASS // 8, 8, 8, CHANNELS), BF16),
         "whiten",
-        (y, odd, *staged),
-        in_hbm=(2, 3, 4, 5),
-        scratch=[*(pltpu.VMEM(t.shape, t.dtype) for t in staged), pltpu.SemaphoreType.DMA((len(staged),))],
+        (y, even, half, near, response, odd),
+        in_hbm=(5,),
+        scratch=[pltpu.VMEM(odd.shape, BF16), pltpu.SemaphoreType.DMA(())],
     )
     owners = BAND // 2
     white = lax.all_to_all(white.reshape(owners, 8, CHANNELS), BOTH, 0, 0, tiled=True)
@@ -217,6 +213,7 @@
         pltpu.VMEM((2 * owners, 128), F32),
         "cross",
         (white.reshape(owners // 2, 16, CHANNELS),),
+        cost=pl.CostEstimate(flops=2 * 10**9, transcendentals=0, bytes_accessed=4 * 10**6),
     )
     cross = lax.all_to_all(cross.reshape(owners, 2, 128), BOTH, 0, 0, tiled=True)
     lagged = kernel_call(

time: 96.6 us -> 95.6 us (0.990)
  Pallas kernels: 7.53 us -> 6.52 us
    pallas_call x3, Pallas kernels: 7.53 us -> 6.52 us  [kernel_call(): pl.pallas_call(kernel, in_specs=[hbm if k in in_hbm else vmem for k in ra...]
  transfers between devices with their start and end apart: 1 -> 1, of which waited for: 1 -> 1; matrix products, arithmetic and copies ran while one was open for 3% -> 2% of each run, Pallas kernels for 0% -> 0%
where the time goes in v5:
time: 95.6 us; the launch traced here: 95.3 us
  blocking collectives  53.2 us (56%)
  waiting for transfers between devices  23.6 us (25%)
  starting transfers between devices  10.2 us (11%)
  Pallas kernels  6.52 us (7%)
  matrix products  1.67 us (2%)
    all_to_all x1, blocking collectives, body(): lax.all_to_all(white.reshape(owners, 8, CHANNELS), BOTH, 0, 0, tiled=True)  33 us
    all_to_all x1, waiting for transfers between devices, body(): y = lax.all_to_all(records, 'chan', 0, 0, tiled=True)  23.6 us
    all_to_all x1, blocking collectives, body(): lax.all_to_all(cross.reshape(owners, 2, 128), BOTH, 0, 0, tiled=True)  20.2 us
    all_to_all x1, starting transfers between devices, body(): y = lax.all_to_all(records, 'chan', 0, 0, tiled=True)  10.2 us
    pallas_call x3, Pallas kernels, kernel_call(): pl.pallas_call(kernel, in_specs=[hbm if k in in_hbm else vmem for k in ra...  6.52 us
  transfers between devices with their start and end apart: 1, of which 1 were waited for; matrix products, arithmetic and copies ran while one was open for 2% of the time, Pallas kernels for 0%

profile of v5, /device:TPU:1, one launch (start us, length us, event | category | flops | bytes accessed | tf_op | source)
XLA Modules:
  0.0 95.3 jit_solution(7166999174619404154)
XLA Ops:
  0.0 0.0 copy-start
  0.0 0.0 copy-start.3
  0.0 0.0 copy-start.4
  0.0 0.0 copy-start.5
  0.0 10.2 %all-to-all-start = ((bf16[32,128,128]{2,1,0:T(8,128)(2,1)}), bf16[32,128,128]{2,1,0:T(8,128)(2,1)S(1)}, u32[]{:S(2)}, u32[]{:S(2)}) async-start(bf16[32,128,128]{2,1,0:T(8,128)(2,1)} %param.9), calls=%async_computation | async-start | bytes 2097152 | tf_op jit(solution)/shard_map/all_to_all | solution.py:192
  10.2 0.0 copy-done
  10.2 1.7 %fusion.resp_ref = f32[1024,128]{1,0:T(8,128)S(1)} fusion(f32[1024,64]{1,0:T(8,128)} %constant.14.clone, f32[64]{0:T(128)S(1)} %copy-done), kind=kOutput, calls=%fused_computation | convolution fusion | flops 100663296 | bytes 786688 | tf_op jit(solution)/shard_map/dot_general | solution.py:194
  11.9 23.6 %all-to-all-done = bf16[32,128,128]{2,1,0:T(8,128)(2,1)S(1)} async-done(((bf16[32,128,128]{2,1,0:T(8,128)(2,1)}), bf16[32,128,128]{2,1,0:T(8,128)(2,1)S(1)}, u32[]{:S(2)}, u32[]{:S(2)}) %all-to-all-start) | async-done | bytes 1048608 | tf_op jit(solution)/shard_map/all_to_all | solution.py:192
  35.5 0.0 copy-done.3
  35.5 0.0 copy-done.4
  35.5 0.0 copy-done.5
  35.5 3.9 %whiten.1 = bf16[2,16,8,8,128]{4,3,2,1,0:T(8,128)(2,1)S(1)} custom-call(bf16[16,256,128]{2,1,0:T(8,128)(2,1)S(1)} %bitcast.7, bf16[512,512]{1,0:T(8,128)(2,1)S(1)} %copy-done.5, bf16[512,512]{1,0:T(8,128)(2,1)S(1)} %copy-done.4, bf16[512,512]{1,0:T(8,128)(2,1)S(1)} %copy-done.3, f32[1024,128]{1,0:T(8,128)S(1)} %fusion.resp_ref, ...), custom_call_target="tpu_custom_call" | custom-call | tf_op jit(solution)/shard_map/whiten/pallas_call | solution.py:178
  39.5 33.0 %all_to_all.15 = bf16[256,8,128]{2,1,0:T(8,128)(2,1)S(1)} all-to-all(bf16[256,8,128]{2,1,0:T(8,128)(2,1)S(1)} %bitcast.8), channel_id=1, replica_groups=mesh['chan'=16,'win'=16] {'win','chan'}, dimensions={0} | all-to-all | bytes 1048576 | tf_op jit(solution)/shard_map/all_to_all | solution.py:210
  72.5 0.0 copy-start.1
  72.5 0.0 copy-start.2
  72.5 1.1 %cross.1 = f32[512,128]{1,0:T(8,128)S(1)} custom-call(bf16[128,16,128]{2,1,0:T(8,128)(2,1)S(1)} %bitcast.10), custom_call_target="tpu_custom_call" | custom-call | flops 2000000000 | bytes 4000000 | tf_op jit(solution)/shard_map/cross/pallas_call | solution.py:178
  73.6 20.2 %all_to_all.16 = f32[256,2,128]{2,1,0:T(2,128)S(1)} all-to-all(f32[256,2,128]{2,1,0:T(2,128)S(1)} %bitcast.11), channel_id=1, replica_groups=mesh['chan'=16,'win'=16] {'win','chan'}, dimensions={0} | all-to-all | bytes 524288 | tf_op jit(solution)/shard_map/all_to_all | solution.py:218
  93.8 0.0 copy-done.1
  93.8 0.0 copy-done.2
  93.8 1.5 %lag.1 = bf16[64,1024]{1,0:T(8,128)(2,1)} custom-call(f32[512,128]{1,0:T(8,128)S(1)} %bitcast.9, bf16[1024,1024]{1,0:T(8,128)(2,1)S(1)} %copy-done.2, bf16[1024,1024]{1,0:T(8,128)(2,1)S(1)} %copy-done.1), custom_call_target="tpu_custom_call" | custom-call | tf_op jit(solution)/shard_map/lag/pallas_call | solution.py:178
Async XLA Ops:
  0.0 10.2 %copy-start = (f32[64]{0:T(128)S(1)}, f32[64]{0:T(128)}, u32[]{:S(2)}) copy-start(f32[64]{0:T(128)} %param.10) | copy-start | bytes 772
  0.0 35.5 %copy-start.3 = (bf16[512,512]{1,0:T(8,128)(2,1)S(1)}, bf16[512,512]{1,0:T(8,128)(2,1)}, u32[]{:S(2)}) copy-start(bf16[512,512]{1,0:T(8,128)(2,1)} %constant.17.clone.near_ref) | copy-start | bytes 1572868
  0.0 35.5 %copy-start.4 = (bf16[512,512]{1,0:T(8,128)(2,1)S(1)}, bf16[512,512]{1,0:T(8,128)(2,1)}, u32[]{:S(2)}) copy-start(bf16[512,512]{1,0:T(8,128)(2,1)} %constant.16.clone.half_ref) | copy-start | bytes 1572868
  0.0 35.5 %copy-start.5 = (bf16[512,512]{1,0:T(8,128)(2,1)S(1)}, bf16[512,512]{1,0:T(8,128)(2,1)}, u32[]{:S(2)}) copy-start(bf16[512,512]{1,0:T(8,128)(2,1)} %constant.15.clone.even_ref) | copy-start | bytes 1572868
  0.0 35.5 %all-to-all-start = ((bf16[32,128,128]{2,1,0:T(8,128)(2,1)}), bf16[32,128,128]{2,1,0:T(8,128)(2,1)S(1)}, u32[]{:S(2)}, u32[]{:S(2)}) async-start(bf16[32,128,128]{2,1,0:T(8,128)(2,1)} %param.9), calls=%async_computation | async-start | bytes 2097152 | tf_op jit(solution)/shard_map/all_to_all | solution.py:192
  72.5 21.3 %copy-start.1 = (bf16[1024,1024]{1,0:T(8,128)(2,1)S(1)}, bf16[1024,1024]{1,0:T(8,128)(2,1)}, u32[]{:S(2)}) copy-start(bf16[1024,1024]{1,0:T(8,128)(2,1)} %constant.20.clone.lo_ref) | copy-start | bytes 6291460
  72.5 21.3 %copy-start.2 = (bf16[1024,1024]{1,0:T(8,128)(2,1)S(1)}, bf16[1024,1024]{1,0:T(8,128)(2,1)}, u32[]{:S(2)}) copy-start(bf16[1024,1024]{1,0:T(8,128)(2,1)} %constant.19.clone.hi_ref) | copy-start | bytes 6291460

commit v6 on v5

--- a/solution.py
+++ b/solution.py
@@ -23,6 +23,7 @@
 QUARTER = LENGTH // RADIX
 PER_CLASS = BAND // RADIX
 
+ORDER = [2 * z + x for z in (0, 4, 1, 5, 2, 6, 3, 7) for x in (0, 1)]
 BF16 = jnp.bfloat16
 F32 = jnp.float32
 
@@ -92,7 +93,7 @@
     blocks = y_ref.shape[0] // RADIX
     sums = [[], [], [], []]
     for j in range(blocks):
-        u = [y_ref[h * blocks + j].astype(F32) for h in range(RADIX)]
+        u = [y_ref[ORDER.index(h * blocks + j)].astype(F32) for h in range(RADIX)]
         even, odd = u[0] + u[2], u[1] + u[3]
         for k, x in enumerate((even + odd, even - odd, u[0] - u[2], u[1] - u[3])):
             sums[k].append(two_terms(x))
@@ -189,7 +190,7 @@
 
 def body(records, fir_taps):
     forward, near, (inv_hi, inv_lo), taps_table = tables()
-    y = lax.all_to_all(records, "chan", 0, 0, tiled=True)
+    y = lax.all_to_all(records, "chan", 0, 0, tiled=True, axis_index_groups=[ORDER])
     y = y.reshape(LENGTH // CHANNELS, 2 * CHANNELS, CHANNELS)
     response = jnp.dot(
         taps_table,

time: 95.6 us -> 95 us (level)
  blocking collectives: 53.2 us -> 50.7 us
  waiting for transfers between devices: 23.6 us -> 25.6 us
    all_to_all x1, blocking collectives: 33 us -> 30.5 us  [body(): lax.all_to_all(white.reshape(owners, 8, CHANNELS), BOTH, 0, 0, tiled=True)]
    all_to_all x1, waiting for transfers between devices: 23.6 us -> 25.6 us  [body(): lax.all_to_all(records, 'chan', 0, 0, tiled=True, axis_index_groups=[ORDER])]
where the time goes in v6:
time: 95 us; the launch traced here: 94.7 us
  blocking collectives  50.7 us (53%)
  waiting for transfers between devices  25.6 us (27%)
  starting transfers between devices  10.2 us (11%)
  Pallas kernels  6.52 us (7%)
  matrix products  1.67 us (2%)
    all_to_all x1, blocking collectives, body(): lax.all_to_all(white.reshape(owners, 8, CHANNELS), BOTH, 0, 0, tiled=True)  30.5 us
    all_to_all x1, waiting for transfers between devices, body(): lax.all_to_all(records, 'chan', 0, 0, tiled=True, axis_index_groups=[ORDER])  25.6 us
    all_to_all x1, blocking collectives, body(): lax.all_to_all(cross.reshape(owners, 2, 128), BOTH, 0, 0, tiled=True)  20.2 us
    all_to_all x1, starting transfers between devices, body(): lax.all_to_all(records, 'chan', 0, 0, tiled=True, axis_index_groups=[ORDER])  10.2 us
    pallas_call x3, Pallas kernels, kernel_call(): pl.pallas_call(kernel, in_specs=[hbm if k in in_hbm else vmem for k in ra...  6.52 us
  transfers between devices with their start and end apart: 1, of which 1 were waited for; matrix products, arithmetic and copies ran while one was open for 2% of the time, Pallas kernels for 0%

profile of v6, /device:TPU:1, one launch (start us, length us, event | category | flops | bytes accessed | tf_op | source)
XLA Modules:
  0.0 94.7 jit_solution(7288514878042741960)
XLA Ops:
  0.0 0.0 copy-start
  0.0 0.0 copy-start.3
  0.0 0.0 copy-start.4
  0.0 0.0 copy-start.5
  0.0 10.2 %all-to-all-start = ((bf16[32,128,128]{2,1,0:T(8,128)(2,1)}), bf16[32,128,128]{2,1,0:T(8,128)(2,1)S(1)}, u32[]{:S(2)}, u32[]{:S(2)}) async-start(bf16[32,128,128]{2,1,0:T(8,128)(2,1)} %param.9), calls=%async_computation | async-start | bytes 2097152 | tf_op jit(solution)/shard_map/all_to_all | solution.py:193
  10.2 0.0 copy-done
  10.2 1.7 %fusion.resp_ref = f32[1024,128]{1,0:T(8,128)S(1)} fusion(f32[1024,64]{1,0:T(8,128)} %constant.14.clone, f32[64]{0:T(128)S(1)} %copy-done), kind=kOutput, calls=%fused_computation | convolution fusion | flops 100663296 | bytes 786688 | tf_op jit(solution)/shard_map/dot_general | solution.py:195
  11.9 25.6 %all-to-all-done = bf16[32,128,128]{2,1,0:T(8,128)(2,1)S(1)} async-done(((bf16[32,128,128]{2,1,0:T(8,128)(2,1)}), bf16[32,128,128]{2,1,0:T(8,128)(2,1)S(1)}, u32[]{:S(2)}, u32[]{:S(2)}) %all-to-all-start) | async-done | bytes 1048608 | tf_op jit(solution)/shard_map/all_to_all | solution.py:193
  37.5 0.0 copy-done.3
  37.5 0.0 copy-done.4
  37.5 0.0 copy-done.5
  37.5 3.9 %whiten.1 = bf16[2,16,8,8,128]{4,3,2,1,0:T(8,128)(2,1)S(1)} custom-call(bf16[16,256,128]{2,1,0:T(8,128)(2,1)S(1)} %bitcast.7, bf16[512,512]{1,0:T(8,128)(2,1)S(1)} %copy-done.5, bf16[512,512]{1,0:T(8,128)(2,1)S(1)} %copy-done.4, bf16[512,512]{1,0:T(8,128)(2,1)S(1)} %copy-done.3, f32[1024,128]{1,0:T(8,128)S(1)} %fusion.resp_ref, ...), custom_call_target="tpu_custom_call" | custom-call | tf_op jit(solution)/shard_map/whiten/pallas_call | solution.py:179
  41.5 30.5 %all_to_all.15 = bf16[256,8,128]{2,1,0:T(8,128)(2,1)S(1)} all-to-all(bf16[256,8,128]{2,1,0:T(8,128)(2,1)S(1)} %bitcast.8), channel_id=1, replica_groups=mesh['chan'=16,'win'=16] {'win','chan'}, dimensions={0} | all-to-all | bytes 1048576 | tf_op jit(solution)/shard_map/all_to_all | solution.py:211
  71.9 0.0 copy-start.1
  71.9 0.0 copy-start.2
  71.9 1.1 %cross.1 = f32[512,128]{1,0:T(8,128)S(1)} custom-call(bf16[128,16,128]{2,1,0:T(8,128)(2,1)S(1)} %bitcast.10), custom_call_target="tpu_custom_call" | custom-call | flops 2000000000 | bytes 4000000 | tf_op jit(solution)/shard_map/cross/pallas_call | solution.py:179
  73.1 20.2 %all_to_all.16 = f32[256,2,128]{2,1,0:T(2,128)S(1)} all-to-all(f32[256,2,128]{2,1,0:T(2,128)S(1)} %bitcast.11), channel_id=1, replica_groups=mesh['chan'=16,'win'=16] {'win','chan'}, dimensions={0} | all-to-all | bytes 524288 | tf_op jit(solution)/shard_map/all_to_all | solution.py:219
  93.3 0.0 copy-done.1
  93.3 0.0 copy-done.2
  93.3 1.5 %lag.1 = bf16[64,1024]{1,0:T(8,128)(2,1)} custom-call(f32[512,128]{1,0:T(8,128)S(1)} %bitcast.9, bf16[1024,1024]{1,0:T(8,128)(2,1)S(1)} %copy-done.2, bf16[1024,1024]{1,0:T(8,128)(2,1)S(1)} %copy-done.1), custom_call_target="tpu_custom_call" | custom-call | tf_op jit(solution)/shard_map/lag/pallas_call | solution.py:179
Async XLA Ops:
  0.0 10.2 %copy-start = (f32[64]{0:T(128)S(1)}, f32[64]{0:T(128)}, u32[]{:S(2)}) copy-start(f32[64]{0:T(128)} %param.10) | copy-start | bytes 772
  0.0 37.5 %copy-start.3 = (bf16[512,512]{1,0:T(8,128)(2,1)S(1)}, bf16[512,512]{1,0:T(8,128)(2,1)}, u32[]{:S(2)}) copy-start(bf16[512,512]{1,0:T(8,128)(2,1)} %constant.17.clone.near_ref) | copy-start | bytes 1572868
  0.0 37.5 %copy-start.4 = (bf16[512,512]{1,0:T(8,128)(2,1)S(1)}, bf16[512,512]{1,0:T(8,128)(2,1)}, u32[]{:S(2)}) copy-start(bf16[512,512]{1,0:T(8,128)(2,1)} %constant.16.clone.half_ref) | copy-start | bytes 1572868
  0.0 37.5 %copy-start.5 = (bf16[512,512]{1,0:T(8,128)(2,1)S(1)}, bf16[512,512]{1,0:T(8,128)(2,1)}, u32[]{:S(2)}) copy-start(bf16[512,512]{1,0:T(8,128)(2,1)} %constant.15.clone.even_ref) | copy-start | bytes 1572868
  0.0 37.5 %all-to-all-start = ((bf16[32,128,128]{2,1,0:T(8,128)(2,1)}), bf16[32,128,128]{2,1,0:T(8,128)(2,1)S(1)}, u32[]{:S(2)}, u32[]{:S(2)}) async-start(bf16[32,128,128]{2,1,0:T(8,128)(2,1)} %param.9), calls=%async_computation | async-start | bytes 2097152 | tf_op jit(solution)/shard_map/all_to_all | solution.py:193
  71.9 21.3 %copy-start.1 = (bf16[1024,1024]{1,0:T(8,128)(2,1)S(1)}, bf16[1024,1024]{1,0:T(8,128)(2,1)}, u32[]{:S(2)}) copy-start(bf16[1024,1024]{1,0:T(8,128)(2,1)} %constant.20.clone.lo_ref) | copy-start | bytes 6291460
  71.9 21.3 %copy-start.2 = (bf16[1024,1024]{1,0:T(8,128)(2,1)S(1)}, bf16[1024,1024]{1,0:T(8,128)(2,1)}, u32[]{:S(2)}) copy-start(bf16[1024,1024]{1,0:T(8,128)(2,1)} %constant.19.clone.hi_ref) | copy-start | bytes 6291460

commit v7 on v6

--- a/solution.py
+++ b/solution.py
@@ -56,9 +56,9 @@
     angles = phases(bins, np.arange(TAPS))
     taps = np.concatenate([np.cos(angles), -np.sin(angles)]).astype(np.float32)
     owned = order.reshape(2, 2, PER_CLASS).transpose(1, 0, 2).reshape(-1)
-    angles = phases(FIRST_BIN + owned, np.arange(2 * LAGS) - LAGS)
+    angles = phases(FIRST_BIN + owned, np.arange(LAGS))
     inverse = np.stack([np.cos(angles), -np.sin(angles)], axis=1) / (WINDOWS * BAND)
-    return forward, near.astype(ml_dtypes.bfloat16), split_table(inverse.reshape(2 * BAND, 2 * LAGS)), taps
+    return forward, near.astype(ml_dtypes.bfloat16), split_table(inverse.reshape(2 * BAND, LAGS)), taps
 
 
 def dot_nt(a, b):
@@ -167,11 +167,23 @@
 
 
 def lag_kernel(c_ref, hi_ref, lo_ref, out_ref):
-    turned = c_ref[...].T
-    hi, lo = two_terms(jnp.concatenate([turned[:64], turned[64:]], axis=1))
+    c = c_ref[...]
+    rows = c.shape[0]
+    row = lax.broadcasted_iota(jnp.int32, c.shape, 0)
+    imag = (row & 1) != 0
+    late = row >= rows // 2
+    low_class = lax.broadcasted_iota(jnp.int32, c.shape, 1) >= c.shape[1] // 2
+    swapped = jnp.where(imag, pltpu.roll(c, 1, 0), pltpu.roll(c, rows - 1, 0))
+    turned = jnp.where(low_class, jnp.where(imag, -swapped, swapped), c)
+    turned = jnp.where(late, -turned, turned)
+    halves = []
+    for x in (c.T, turned.T):
+        halves.append(jnp.concatenate([x[:64], x[64:]], axis=1))
+    hi, lo = two_terms(jnp.concatenate(halves, axis=0))
     both = dot_nn(jnp.concatenate([hi, lo], axis=0), hi_ref[...])
-    total = both[:64] + (both[64:] + dot_nn(hi, lo_ref[...]))
-    out_ref[...] = total.astype(BF16)
+    total = both[:128] + (both[128:] + dot_nn(hi, lo_ref[...]))
+    out_ref[:, :LAGS] = total[64:].astype(BF16)
+    out_ref[:, LAGS:] = total[:64].astype(BF16)
 
 
 def kernel_call(kernel, out_shape, name, args, in_hbm=(), scratch=(), cost=None, limit=24):

time: 95 us -> 94.9 us (level)
  no operation moved by 1% of the time
where the time goes in v7:
time: 94.9 us; the launch traced here: 94.6 us
  blocking collectives  50.7 us (53%)
  waiting for transfers between devices  25.6 us (27%)
  starting transfers between devices  10.2 us (11%)
  Pallas kernels  6.39 us (7%)
  matrix products  1.67 us (2%)
    all_to_all x1, blocking collectives, body(): lax.all_to_all(white.reshape(owners, 8, CHANNELS), BOTH, 0, 0, tiled=True)  30.5 us
    all_to_all x1, waiting for transfers between devices, body(): lax.all_to_all(records, 'chan', 0, 0, tiled=True, axis_index_groups=[ORDER])  25.6 us
    all_to_all x1, blocking collectives, body(): lax.all_to_all(cross.reshape(owners, 2, 128), BOTH, 0, 0, tiled=True)  20.2 us
    all_to_all x1, starting transfers between devices, body(): lax.all_to_all(records, 'chan', 0, 0, tiled=True, axis_index_groups=[ORDER])  10.2 us
    pallas_call x3, Pallas kernels, kernel_call(): pl.pallas_call(kernel, in_specs=[hbm if k in in_hbm else vmem for k in ra...  6.39 us
  transfers between devices with their start and end apart: 1, of which 1 were waited for; matrix products, arithmetic and copies ran while one was open for 2% of the time, Pallas kernels for 0%

profile of v7, /device:TPU:1, one launch (start us, length us, event | category | flops | bytes accessed | tf_op | source)
XLA Modules:
  0.0 94.6 jit_solution(1250612357400243824)
XLA Ops:
  0.0 0.0 copy-start
  0.0 0.0 copy-start.3
  0.0 0.0 copy-start.4
  0.0 0.0 copy-start.5
  0.0 10.2 %all-to-all-start = ((bf16[32,128,128]{2,1,0:T(8,128)(2,1)}), bf16[32,128,128]{2,1,0:T(8,128)(2,1)S(1)}, u32[]{:S(2)}, u32[]{:S(2)}) async-start(bf16[32,128,128]{2,1,0:T(8,128)(2,1)} %param.9), calls=%async_computation | async-start | bytes 2097152 | tf_op jit(solution)/shard_map/all_to_all | solution.py:205
  10.2 0.0 copy-done
  10.2 1.7 %fusion.resp_ref = f32[1024,128]{1,0:T(8,128)S(1)} fusion(f32[1024,64]{1,0:T(8,128)} %constant.14.clone, f32[64]{0:T(128)S(1)} %copy-done), kind=kOutput, calls=%fused_computation | convolution fusion | flops 100663296 | bytes 786688 | tf_op jit(solution)/shard_map/dot_general | solution.py:207
  11.9 25.6 %all-to-all-done = bf16[32,128,128]{2,1,0:T(8,128)(2,1)S(1)} async-done(((bf16[32,128,128]{2,1,0:T(8,128)(2,1)}), bf16[32,128,128]{2,1,0:T(8,128)(2,1)S(1)}, u32[]{:S(2)}, u32[]{:S(2)}) %all-to-all-start) | async-done | bytes 1048608 | tf_op jit(solution)/shard_map/all_to_all | solution.py:205
  37.5 0.0 copy-done.3
  37.5 0.0 copy-done.4
  37.5 0.0 copy-done.5
  37.5 3.9 %whiten.1 = bf16[2,16,8,8,128]{4,3,2,1,0:T(8,128)(2,1)S(1)} custom-call(bf16[16,256,128]{2,1,0:T(8,128)(2,1)S(1)} %bitcast.7, bf16[512,512]{1,0:T(8,128)(2,1)S(1)} %copy-done.5, bf16[512,512]{1,0:T(8,128)(2,1)S(1)} %copy-done.4, bf16[512,512]{1,0:T(8,128)(2,1)S(1)} %copy-done.3, f32[1024,128]{1,0:T(8,128)S(1)} %fusion.resp_ref, ...), custom_call_target="tpu_custom_call" | custom-call | tf_op jit(solution)/shard_map/whiten/pallas_call | solution.py:191
  41.5 30.5 %all_to_all.15 = bf16[256,8,128]{2,1,0:T(8,128)(2,1)S(1)} all-to-all(bf16[256,8,128]{2,1,0:T(8,128)(2,1)S(1)} %bitcast.8), channel_id=1, replica_groups=mesh['chan'=16,'win'=16] {'win','chan'}, dimensions={0} | all-to-all | bytes 1048576 | tf_op jit(solution)/shard_map/all_to_all | solution.py:223
  71.9 0.0 copy-start.1
  71.9 0.0 copy-start.2
  71.9 1.1 %cross.1 = f32[512,128]{1,0:T(8,128)S(1)} custom-call(bf16[128,16,128]{2,1,0:T(8,128)(2,1)S(1)} %bitcast.10), custom_call_target="tpu_custom_call" | custom-call | flops 2000000000 | bytes 4000000 | tf_op jit(solution)/shard_map/cross/pallas_call | solution.py:191
  73.1 20.2 %all_to_all.16 = f32[256,2,128]{2,1,0:T(2,128)S(1)} all-to-all(f32[256,2,128]{2,1,0:T(2,128)S(1)} %bitcast.11), channel_id=1, replica_groups=mesh['chan'=16,'win'=16] {'win','chan'}, dimensions={0} | all-to-all | bytes 524288 | tf_op jit(solution)/shard_map/all_to_all | solution.py:231
  93.3 0.0 copy-done.1
  93.3 0.0 copy-done.2
  93.3 1.3 %lag.1 = bf16[64,1024]{1,0:T(8,128)(2,1)} custom-call(f32[512,128]{1,0:T(8,128)S(1)} %bitcast.9, bf16[1024,512]{1,0:T(8,128)(2,1)S(1)} %copy-done.2, bf16[1024,512]{1,0:T(8,128)(2,1)S(1)} %copy-done.1), custom_call_target="tpu_custom_call" | custom-call | tf_op jit(solution)/shard_map/lag/pallas_call | solution.py:191
Async XLA Ops:
  0.0 10.2 %copy-start = (f32[64]{0:T(128)S(1)}, f32[64]{0:T(128)}, u32[]{:S(2)}) copy-start(f32[64]{0:T(128)} %param.10) | copy-start | bytes 772
  0.0 37.5 %copy-start.3 = (bf16[512,512]{1,0:T(8,128)(2,1)S(1)}, bf16[512,512]{1,0:T(8,128)(2,1)}, u32[]{:S(2)}) copy-start(bf16[512,512]{1,0:T(8,128)(2,1)} %constant.17.clone.near_ref) | copy-start | bytes 1572868
  0.0 37.5 %copy-start.4 = (bf16[512,512]{1,0:T(8,128)(2,1)S(1)}, bf16[512,512]{1,0:T(8,128)(2,1)}, u32[]{:S(2)}) copy-start(bf16[512,512]{1,0:T(8,128)(2,1)} %constant.16.clone.half_ref) | copy-start | bytes 1572868
  0.0 37.5 %copy-start.5 = (bf16[512,512]{1,0:T(8,128)(2,1)S(1)}, bf16[512,512]{1,0:T(8,128)(2,1)}, u32[]{:S(2)}) copy-start(bf16[512,512]{1,0:T(8,128)(2,1)} %constant.15.clone.even_ref) | copy-start | bytes 1572868
  0.0 37.5 %all-to-all-start = ((bf16[32,128,128]{2,1,0:T(8,128)(2,1)}), bf16[32,128,128]{2,1,0:T(8,128)(2,1)S(1)}, u32[]{:S(2)}, u32[]{:S(2)}) async-start(bf16[32,128,128]{2,1,0:T(8,128)(2,1)} %param.9), calls=%async_computation | async-start | bytes 2097152 | tf_op jit(solution)/shard_map/all_to_all | solution.py:205
  71.9 21.3 %copy-start.1 = (bf16[1024,512]{1,0:T(8,128)(2,1)S(1)}, bf16[1024,512]{1,0:T(8,128)(2,1)}, u32[]{:S(2)}) copy-start(bf16[1024,512]{1,0:T(8,128)(2,1)} %constant.20.clone.lo_ref) | copy-start | bytes 3145732
  71.9 21.3 %copy-start.2 = (bf16[1024,512]{1,0:T(8,128)(2,1)S(1)}, bf16[1024,512]{1,0:T(8,128)(2,1)}, u32[]{:S(2)}) copy-start(bf16[1024,512]{1,0:T(8,128)(2,1)} %constant.19.clone.hi_ref) | copy-start | bytes 3145732

commit v8 on v6

--- a/solution.py
+++ b/solution.py
@@ -56,9 +56,9 @@
     angles = phases(bins, np.arange(TAPS))
     taps = np.concatenate([np.cos(angles), -np.sin(angles)]).astype(np.float32)
     owned = order.reshape(2, 2, PER_CLASS).transpose(1, 0, 2).reshape(-1)
-    angles = phases(FIRST_BIN + owned, np.arange(2 * LAGS) - LAGS)
+    angles = phases(FIRST_BIN + owned, np.arange(LAGS))
     inverse = np.stack([np.cos(angles), -np.sin(angles)], axis=1) / (WINDOWS * BAND)
-    return forward, near.astype(ml_dtypes.bfloat16), split_table(inverse.reshape(2 * BAND, 2 * LAGS)), taps
+    return forward, near.astype(ml_dtypes.bfloat16), split_table(inverse.reshape(2 * BAND, LAGS)), taps
 
 
 def dot_nt(a, b):
@@ -166,20 +166,41 @@
                 out_ref[pl.ds(start, 8, stride=32), :] = a[c * 8 : c * 8 + 8]
 
 
-def lag_kernel(c_ref, hi_ref, lo_ref, out_ref):
+def lag_kernel(c_ref, hi_ref, lo_ref, out_hbm, out_ref, sems):
     turned = c_ref[...].T
-    hi, lo = two_terms(jnp.concatenate([turned[:64], turned[64:]], axis=1))
-    both = dot_nn(jnp.concatenate([hi, lo], axis=0), hi_ref[...])
-    total = both[:64] + (both[64:] + dot_nn(hi, lo_ref[...]))
-    out_ref[...] = total.astype(BF16)
-
-
-def kernel_call(kernel, out_shape, name, args, in_hbm=(), scratch=(), cost=None, limit=24):
+    c = jnp.concatenate([turned[:64], turned[64:]], axis=1)
+    size = c.shape[1]
+    lane = lax.broadcasted_iota(jnp.int32, c.shape, 1)
+    imag = (lane & 1) != 0
+    low_class = lane >= size // 2
+    late = (lane & (size // 4)) != 0
+    swapped = jnp.where(imag, pltpu.roll(c, 1, 1), pltpu.roll(c, size - 1, 1))
+    turned = jnp.where(low_class, jnp.where(imag, -swapped, swapped), c)
+    turned = jnp.where(late, -turned, turned)
+    hi, lo = two_terms(jnp.concatenate([c, turned], axis=0))
+    lhs = jnp.concatenate([hi, lo], axis=0)
+    half = LAGS // 2
+    copies = []
+    for k in range(2):
+        cols = pl.ds(k * half, half)
+        both = dot_nn(lhs, hi_ref[:, cols])
+        total = both[:128] + (both[128:] + dot_nn(hi, lo_ref[:, cols]))
+        for part in range(2):
+            cols = pl.ds((1 - part) * LAGS + k * half, half)
+            out_ref[:, cols] = total[64 * part : 64 * part + 64].astype(BF16)
+            copy = pltpu.make_async_copy(out_ref.at[:, cols], out_hbm.at[:, cols], sems.at[2 * k + part])
+            copy.start()
+            copies.append(copy)
+    for copy in copies:
+        copy.wait()
+
+
+def kernel_call(kernel, out_shape, name, args, in_hbm=(), scratch=(), cost=None, limit=24, out_hbm=False):
     vmem, hbm = pl.BlockSpec(memory_space=pltpu.VMEM), pl.BlockSpec(memory_space=pl.ANY)
     return pl.pallas_call(
         kernel,
         in_specs=[hbm if k in in_hbm else vmem for k in range(len(args))],
-        out_specs=vmem,
+        out_specs=hbm if out_hbm else vmem,
         out_shape=out_shape,
         scratch_shapes=scratch,
         name=name,
@@ -222,6 +243,8 @@
         jax.ShapeDtypeStruct((64, 2 * LAGS), BF16),
         "lag",
         (cross.reshape(2 * owners, 128), inv_hi, inv_lo),
+        scratch=[pltpu.VMEM((64, 2 * LAGS), BF16), pltpu.SemaphoreType.DMA((4,))],
+        out_hbm=True,
     )
     return lagged.reshape(8, 8, 2 * LAGS)
 

time: 95 us -> 94.9 us (level)
  no operation moved by 1% of the time
where the time goes in v8:
time: 94.9 us; the launch traced here: 94.6 us
  blocking collectives  50.7 us (53%)
  waiting for transfers between devices  25.6 us (27%)
  starting transfers between devices  10.2 us (11%)
  Pallas kernels  6.35 us (7%)
  matrix products  1.67 us (2%)
    all_to_all x1, blocking collectives, body(): lax.all_to_all(white.reshape(owners, 8, CHANNELS), BOTH, 0, 0, tiled=True)  30.5 us
    all_to_all x1, waiting for transfers between devices, body(): lax.all_to_all(records, 'chan', 0, 0, tiled=True, axis_index_groups=[ORDER])  25.6 us
    all_to_all x1, blocking collectives, body(): lax.all_to_all(cross.reshape(owners, 2, 128), BOTH, 0, 0, tiled=True)  20.2 us
    all_to_all x1, starting transfers between devices, body(): lax.all_to_all(records, 'chan', 0, 0, tiled=True, axis_index_groups=[ORDER])  10.2 us
    pallas_call x3, Pallas kernels, kernel_call(): pl.pallas_call(kernel, in_specs=[hbm if k in in_hbm else vmem for k in ra...  6.35 us
  transfers between devices with their start and end apart: 1, of which 1 were waited for; matrix products, arithmetic and copies ran while one was open for 2% of the time, Pallas kernels for 0%

profile of v8, /device:TPU:1, one launch (start us, length us, event | category | flops | bytes accessed | tf_op | source)
XLA Modules:
  0.0 94.6 jit_solution(12080891923291652634)
XLA Ops:
  0.0 0.0 copy-start
  0.0 0.0 copy-start.3
  0.0 0.0 copy-start.4
  0.0 0.0 copy-start.5
  0.0 10.2 %all-to-all-start = ((bf16[32,128,128]{2,1,0:T(8,128)(2,1)}), bf16[32,128,128]{2,1,0:T(8,128)(2,1)S(1)}, u32[]{:S(2)}, u32[]{:S(2)}) async-start(bf16[32,128,128]{2,1,0:T(8,128)(2,1)} %param.9), calls=%async_computation | async-start | bytes 2097152 | tf_op jit(solution)/shard_map/all_to_all | solution.py:214
  10.2 0.0 copy-done
  10.2 1.7 %fusion.resp_ref = f32[1024,128]{1,0:T(8,128)S(1)} fusion(f32[1024,64]{1,0:T(8,128)} %constant.14.clone, f32[64]{0:T(128)S(1)} %copy-done), kind=kOutput, calls=%fused_computation | convolution fusion | flops 100663296 | bytes 786688 | tf_op jit(solution)/shard_map/dot_general | solution.py:216
  11.9 25.6 %all-to-all-done = bf16[32,128,128]{2,1,0:T(8,128)(2,1)S(1)} async-done(((bf16[32,128,128]{2,1,0:T(8,128)(2,1)}), bf16[32,128,128]{2,1,0:T(8,128)(2,1)S(1)}, u32[]{:S(2)}, u32[]{:S(2)}) %all-to-all-start) | async-done | bytes 1048608 | tf_op jit(solution)/shard_map/all_to_all | solution.py:214
  37.5 0.0 copy-done.3
  37.5 0.0 copy-done.4
  37.5 0.0 copy-done.5
  37.5 3.9 %whiten.1 = bf16[2,16,8,8,128]{4,3,2,1,0:T(8,128)(2,1)S(1)} custom-call(bf16[16,256,128]{2,1,0:T(8,128)(2,1)S(1)} %bitcast.7, bf16[512,512]{1,0:T(8,128)(2,1)S(1)} %copy-done.5, bf16[512,512]{1,0:T(8,128)(2,1)S(1)} %copy-done.4, bf16[512,512]{1,0:T(8,128)(2,1)S(1)} %copy-done.3, f32[1024,128]{1,0:T(8,128)S(1)} %fusion.resp_ref, ...), custom_call_target="tpu_custom_call" | custom-call | tf_op jit(solution)/shard_map/whiten/pallas_call | solution.py:200
  41.5 30.5 %all_to_all.15 = bf16[256,8,128]{2,1,0:T(8,128)(2,1)S(1)} all-to-all(bf16[256,8,128]{2,1,0:T(8,128)(2,1)S(1)} %bitcast.8), channel_id=1, replica_groups=mesh['chan'=16,'win'=16] {'win','chan'}, dimensions={0} | all-to-all | bytes 1048576 | tf_op jit(solution)/shard_map/all_to_all | solution.py:232
  71.9 0.0 copy-start.1
  71.9 0.0 copy-start.2
  71.9 1.1 %cross.1 = f32[512,128]{1,0:T(8,128)S(1)} custom-call(bf16[128,16,128]{2,1,0:T(8,128)(2,1)S(1)} %bitcast.10), custom_call_target="tpu_custom_call" | custom-call | flops 2000000000 | bytes 4000000 | tf_op jit(solution)/shard_map/cross/pallas_call | solution.py:200
  73.1 20.2 %all_to_all.16 = f32[256,2,128]{2,1,0:T(2,128)S(1)} all-to-all(f32[256,2,128]{2,1,0:T(2,128)S(1)} %bitcast.11), channel_id=1, replica_groups=mesh['chan'=16,'win'=16] {'win','chan'}, dimensions={0} | all-to-all | bytes 524288 | tf_op jit(solution)/shard_map/all_to_all | solution.py:240
  93.3 0.0 copy-done.1
  93.3 0.0 copy-done.2
  93.3 1.3 %lag.1 = bf16[64,1024]{1,0:T(8,128)(2,1)} custom-call(f32[512,128]{1,0:T(8,128)S(1)} %bitcast.9, bf16[1024,512]{1,0:T(8,128)(2,1)S(1)} %copy-done.2, bf16[1024,512]{1,0:T(8,128)(2,1)S(1)} %copy-done.1), custom_call_target="tpu_custom_call" | custom-call | tf_op jit(solution)/shard_map/lag/pallas_call | solution.py:200
Async XLA Ops:
  0.0 10.2 %copy-start = (f32[64]{0:T(128)S(1)}, f32[64]{0:T(128)}, u32[]{:S(2)}) copy-start(f32[64]{0:T(128)} %param.10) | copy-start | bytes 772
  0.0 37.5 %copy-start.3 = (bf16[512,512]{1,0:T(8,128)(2,1)S(1)}, bf16[512,512]{1,0:T(8,128)(2,1)}, u32[]{:S(2)}) copy-start(bf16[512,512]{1,0:T(8,128)(2,1)} %constant.17.clone.near_ref) | copy-start | bytes 1572868
  0.0 37.5 %copy-start.4 = (bf16[512,512]{1,0:T(8,128)(2,1)S(1)}, bf16[512,512]{1,0:T(8,128)(2,1)}, u32[]{:S(2)}) copy-start(bf16[512,512]{1,0:T(8,128)(2,1)} %constant.16.clone.half_ref) | copy-start | bytes 1572868
  0.0 37.5 %copy-start.5 = (bf16[512,512]{1,0:T(8,128)(2,1)S(1)}, bf16[512,512]{1,0:T(8,128)(2,1)}, u32[]{:S(2)}) copy-start(bf16[512,512]{1,0:T(8,128)(2,1)} %constant.15.clone.even_ref) | copy-start | bytes 1572868
  0.0 37.5 %all-to-all-start = ((bf16[32,128,128]{2,1,0:T(8,128)(2,1)}), bf16[32,128,128]{2,1,0:T(8,128)(2,1)S(1)}, u32[]{:S(2)}, u32[]{:S(2)}) async-start(bf16[32,128,128]{2,1,0:T(8,128)(2,1)} %param.9), calls=%async_computation | async-start | bytes 2097152 | tf_op jit(solution)/shard_map/all_to_all | solution.py:214
  71.9 21.3 %copy-start.1 = (bf16[1024,512]{1,0:T(8,128)(2,1)S(1)}, bf16[1024,512]{1,0:T(8,128)(2,1)}, u32[]{:S(2)}) copy-start(bf16[1024,512]{1,0:T(8,128)(2,1)} %constant.20.clone.lo_ref) | copy-start | bytes 3145732
  71.9 21.3 %copy-start.2 = (bf16[1024,512]{1,0:T(8,128)(2,1)S(1)}, bf16[1024,512]{1,0:T(8,128)(2,1)}, u32[]{:S(2)}) copy-start(bf16[1024,512]{1,0:T(8,128)(2,1)} %constant.19.clone.hi_ref) | copy-start | bytes 3145732

commit v9 on v7

--- a/solution.py
+++ b/solution.py
@@ -88,8 +88,13 @@
 def whiten_kernel(
     y_ref, even_ref, half_ref, near_ref, resp_ref, odd_hbm, out_ref, odd_ref, sem
 ):
-    copy = pltpu.make_async_copy(odd_hbm, odd_ref, sem)
-    copy.start()
+    part = odd_ref.shape[0] // 2
+    copies = [
+        pltpu.make_async_copy(odd_hbm.at[pl.ds(k * part, part)], odd_ref.at[pl.ds(k * part, part)], sem.at[k])
+        for k in range(2)
+    ]
+    for copy in copies:
+        copy.start()
     blocks = y_ref.shape[0] // RADIX
     sums = [[], [], [], []]
     for j in range(blocks):
@@ -104,9 +109,13 @@
         hi, lo = inputs[k]
         rows = ref.shape[0] // 2
         if k == 2:
-            copy.wait()
-        both = dot_nt(ref[...], hi)
-        spec[k] = both[:rows] + both[rows:] + dot_nt(ref[:rows], lo)
+            copies[0].wait()
+            first = dot_nt(ref[:rows], hi) + dot_nt(ref[:rows], lo)
+            copies[1].wait()
+            spec[k] = first + dot_nt(ref[rows:], hi)
+        else:
+            both = dot_nt(ref[...], hi)
+            spec[k] = both[:rows] + both[rows:] + dot_nt(ref[:rows], lo)
     m = PER_CLASS
     spec_re = jnp.concatenate([spec[0][:m], spec[2][:m], spec[1][:m], spec[2][2 * m : 3 * m]])
     spec_im = jnp.concatenate([spec[0][m:], spec[2][m : 2 * m], spec[1][m:], spec[2][3 * m :]])
@@ -217,7 +226,7 @@
         "whiten",
         (y, even, half, near, response, odd),
         in_hbm=(5,),
-        scratch=[pltpu.VMEM(odd.shape, BF16), pltpu.SemaphoreType.DMA(())],
+        scratch=[pltpu.VMEM(odd.shape, BF16), pltpu.SemaphoreType.DMA((2,))],
     )
     owners = BAND // 2
     white = lax.all_to_all(white.reshape(owners, 8, CHANNELS), BOTH, 0, 0, tiled=True)

time: 94.9 us -> 94.9 us (level)
  no operation moved by 1% of the time
where the time goes in v9:
time: 94.9 us; the launch traced here: 94.6 us
  blocking collectives  50.7 us (53%)
  waiting for transfers between devices  25.6 us (27%)
  starting transfers between devices  10.2 us (11%)
  Pallas kernels  6.37 us (7%)
  matrix products  1.67 us (2%)
    all_to_all x1, blocking collectives, body(): lax.all_to_all(white.reshape(owners, 8, CHANNELS), BOTH, 0, 0, tiled=True)  30.5 us
    all_to_all x1, waiting for transfers between devices, body(): lax.all_to_all(records, 'chan', 0, 0, tiled=True, axis_index_groups=[ORDER])  25.6 us
    all_to_all x1, blocking collectives, body(): lax.all_to_all(cross.reshape(owners, 2, 128), BOTH, 0, 0, tiled=True)  20.2 us
    all_to_all x1, starting transfers between devices, body(): lax.all_to_all(records, 'chan', 0, 0, tiled=True, axis_index_groups=[ORDER])  10.2 us
    pallas_call x3, Pallas kernels, kernel_call(): pl.pallas_call(kernel, in_specs=[hbm if k in in_hbm else vmem for k in ra...  6.37 us
  transfers between devices with their start and end apart: 1, of which 1 were waited for; matrix products, arithmetic and copies ran while one was open for 2% of the time, Pallas kernels for 0%

profile of v9, /device:TPU:1, one launch (start us, length us, event | category | flops | bytes accessed | tf_op | source)
XLA Modules:
  0.0 94.6 jit_solution(3293111007705989371)
XLA Ops:
  0.0 0.0 copy-start
  0.0 0.0 copy-start.3
  0.0 0.0 copy-start.4
  0.0 0.0 copy-start.5
  0.0 10.2 %all-to-all-start = ((bf16[32,128,128]{2,1,0:T(8,128)(2,1)}), bf16[32,128,128]{2,1,0:T(8,128)(2,1)S(1)}, u32[]{:S(2)}, u32[]{:S(2)}) async-start(bf16[32,128,128]{2,1,0:T(8,128)(2,1)} %param.9), calls=%async_computation | async-start | bytes 2097152 | tf_op jit(solution)/shard_map/all_to_all | solution.py:214
  10.2 0.0 copy-done
  10.2 1.7 %fusion.resp_ref = f32[1024,128]{1,0:T(8,128)S(1)} fusion(f32[1024,64]{1,0:T(8,128)} %constant.14.clone, f32[64]{0:T(128)S(1)} %copy-done), kind=kOutput, calls=%fused_computation | convolution fusion | flops 100663296 | bytes 786688 | tf_op jit(solution)/shard_map/dot_general | solution.py:216
  11.9 25.6 %all-to-all-done = bf16[32,128,128]{2,1,0:T(8,128)(2,1)S(1)} async-done(((bf16[32,128,128]{2,1,0:T(8,128)(2,1)}), bf16[32,128,128]{2,1,0:T(8,128)(2,1)S(1)}, u32[]{:S(2)}, u32[]{:S(2)}) %all-to-all-start) | async-done | bytes 1048608 | tf_op jit(solution)/shard_map/all_to_all | solution.py:214
  37.5 0.0 copy-done.3
  37.5 0.0 copy-done.4
  37.5 0.0 copy-done.5
  37.5 3.9 %whiten.1 = bf16[2,16,8,8,128]{4,3,2,1,0:T(8,128)(2,1)S(1)} custom-call(bf16[16,256,128]{2,1,0:T(8,128)(2,1)S(1)} %bitcast.7, bf16[512,512]{1,0:T(8,128)(2,1)S(1)} %copy-done.5, bf16[512,512]{1,0:T(8,128)(2,1)S(1)} %copy-done.4, bf16[512,512]{1,0:T(8,128)(2,1)S(1)} %copy-done.3, f32[1024,128]{1,0:T(8,128)S(1)} %fusion.resp_ref, ...), custom_call_target="tpu_custom_call" | custom-call | tf_op jit(solution)/shard_map/whiten/pallas_call | solution.py:200
  41.4 30.5 %all_to_all.15 = bf16[256,8,128]{2,1,0:T(8,128)(2,1)S(1)} all-to-all(bf16[256,8,128]{2,1,0:T(8,128)(2,1)S(1)} %bitcast.8), channel_id=1, replica_groups=mesh['chan'=16,'win'=16] {'win','chan'}, dimensions={0} | all-to-all | bytes 1048576 | tf_op jit(solution)/shard_map/all_to_all | solution.py:232
  71.9 0.0 copy-start.1
  71.9 0.0 copy-start.2
  71.9 1.1 %cross.1 = f32[512,128]{1,0:T(8,128)S(1)} custom-call(bf16[128,16,128]{2,1,0:T(8,128)(2,1)S(1)} %bitcast.10), custom_call_target="tpu_custom_call" | custom-call | flops 2000000000 | bytes 4000000 | tf_op jit(solution)/shard_map/cross/pallas_call | solution.py:200
  73.0 20.2 %all_to_all.16 = f32[256,2,128]{2,1,0:T(2,128)S(1)} all-to-all(f32[256,2,128]{2,1,0:T(2,128)S(1)} %bitcast.11), channel_id=1, replica_groups=mesh['chan'=16,'win'=16] {'win','chan'}, dimensions={0} | all-to-all | bytes 524288 | tf_op jit(solution)/shard_map/all_to_all | solution.py:240
  93.2 0.0 copy-done.1
  93.2 0.0 copy-done.2
  93.2 1.3 %lag.1 = bf16[64,1024]{1,0:T(8,128)(2,1)} custom-call(f32[512,128]{1,0:T(8,128)S(1)} %bitcast.9, bf16[1024,512]{1,0:T(8,128)(2,1)S(1)} %copy-done.2, bf16[1024,512]{1,0:T(8,128)(2,1)S(1)} %copy-done.1), custom_call_target="tpu_custom_call" | custom-call | tf_op jit(solution)/shard_map/lag/pallas_call | solution.py:200
Async XLA Ops:
  0.0 10.2 %copy-start = (f32[64]{0:T(128)S(1)}, f32[64]{0:T(128)}, u32[]{:S(2)}) copy-start(f32[64]{0:T(128)} %param.10) | copy-start | bytes 772
  0.0 37.5 %copy-start.3 = (bf16[512,512]{1,0:T(8,128)(2,1)S(1)}, bf16[512,512]{1,0:T(8,128)(2,1)}, u32[]{:S(2)}) copy-start(bf16[512,512]{1,0:T(8,128)(2,1)} %constant.17.clone.near_ref) | copy-start | bytes 1572868
  0.0 37.5 %copy-start.4 = (bf16[512,512]{1,0:T(8,128)(2,1)S(1)}, bf16[512,512]{1,0:T(8,128)(2,1)}, u32[]{:S(2)}) copy-start(bf16[512,512]{1,0:T(8,128)(2,1)} %constant.16.clone.half_ref) | copy-start | bytes 1572868
  0.0 37.5 %copy-start.5 = (bf16[512,512]{1,0:T(8,128)(2,1)S(1)}, bf16[512,512]{1,0:T(8,128)(2,1)}, u32[]{:S(2)}) copy-start(bf16[512,512]{1,0:T(8,128)(2,1)} %constant.15.clone.even_ref) | copy-start | bytes 1572868
  0.0 37.5 %all-to-all-start = ((bf16[32,128,128]{2,1,0:T(8,128)(2,1)}), bf16[32,128,128]{2,1,0:T(8,128)(2,1)S(1)}, u32[]{:S(2)}, u32[]{:S(2)}) async-start(bf16[32,128,128]{2,1,0:T(8,128)(2,1)} %param.9), calls=%async_computation | async-start | bytes 2097152 | tf_op jit(solution)/shard_map/all_to_all | solution.py:214
  71.9 21.3 %copy-start.1 = (bf16[1024,512]{1,0:T(8,128)(2,1)S(1)}, bf16[1024,512]{1,0:T(8,128)(2,1)}, u32[]{:S(2)}) copy-start(bf16[1024,512]{1,0:T(8,128)(2,1)} %constant.20.clone.lo_ref) | copy-start | bytes 3145732
  71.9 21.3 %copy-start.2 = (bf16[1024,512]{1,0:T(8,128)(2,1)S(1)}, bf16[1024,512]{1,0:T(8,128)(2,1)}, u32[]{:S(2)}) copy-start(bf16[1024,512]{1,0:T(8,128)(2,1)} %constant.19.clone.hi_ref) | copy-start | bytes 3145732
